TPU v7x, 128 devices: a whole 4x4x4 slice. The times are simulated.
128 devices in a mesh: wide: 32 (over z, y, core), narrow: 4 (over x).
Axes of the slice: x: 4, y: 4, z: 4, core: 2. Of those that a mesh axis runs over, the one named last changes fastest.
Arguments:
- slab: float32 [4, 512, 512, 256], P(None, 'narrow', 'wide'), may hold values from -180 to 180
- factor: float32 [512, 64], replicated, may hold values from -0.25 to 0.25
Outputs:
- r_factor: float32 [512, 512], replicated
- core: float32 [4, 64, 512, 256], P(None, None, 'wide', 'narrow')
All inputs are finite; a program needn't handle non-finite values.
Results may differ from a plain program's by a relative error of at most 0.00007.
Values sent between devices are 32-bit elements; how exact they have to be, the bound alone decides.
No kernel may reach another device: no remote copies, remote signals or barrier semaphores. Data moves between devices by JAX's collectives and lax.ppermute only.
A program may use at most 256 MiB of HBM per device.

v0:
```python
import functools
import jax
import jax.numpy as jnp
from jax import lax
from jax.experimental import pallas as pl
from jax.experimental.pallas import tpu as pltpu
from jax.sharding import Mesh, PartitionSpec as P

HI = lax.Precision.HIGHEST
BLOCKS = [(i, j) for i in range(4) for j in range(i, 4)]
SHIFTS = (1, 3, 2)
HALF = 640
WIDE = ("z", "y", "core")
F32 = jnp.float32
BF16 = jnp.bfloat16


def ring(size, shift):
    return [(i, (i + shift) % size) for i in range(size)]


def pack_kernel(x0_ref, x1_ref, *outs):
    n = lax.axis_index("narrow")
    rows = x0_ref.shape[0] // 16
    parts = len(outs) // 4
    depth = 8 // parts
    low = lax.broadcasted_iota(jnp.int32, (rows, 128), 1) < 64

    def body(k):
        for part in range(parts):

            @pl.loop(0, depth)
            def _(a):
                at = part * depth + a
                for tile, x_ref in enumerate((x0_ref, x1_ref)):
                    lo = x_ref[pl.ds(at, rows, stride=16), :]
                    hi = x_ref[pl.ds(at + 8, rows, stride=16), :]
                    even = jnp.where(low, lo, pltpu.roll(hi, 64, 1))
                    odd = jnp.where(low, pltpu.roll(lo, 64, 1), hi)
                    outs[4 * part + (2 * tile - k) % 4][a] = even
                    outs[4 * part + (2 * tile + 1 - k) % 4][a] = odd

    for k in range(4):
        pl.when(n == k)(functools.partial(body, k))


def pack(slab, comp, parts):
    rows = 1024
    depth = 8 // parts
    outs = pl.pallas_call(
        pack_kernel,
        grid=(2,),
        in_specs=[
            pl.BlockSpec((None, rows, 128), lambda i: (comp, i, 0)),
            pl.BlockSpec((None, rows, 128), lambda i: (comp, i, 1)),
        ],
        out_specs=[pl.BlockSpec((depth, rows // 16, 128), lambda i: (0, i, 0))] * (4 * parts),
        out_shape=[jax.ShapeDtypeStruct((depth, 128, 128), F32)] * (4 * parts),
        cost_estimate=pl.CostEstimate(
            flops=1 << 20, bytes_accessed=4 << 20, transcendentals=0
        ),
        name="pack",
    )(slab, slab)
    return [outs[4 * k:4 * k + 4] for k in range(parts)]


def split(x):
    h = x.astype(BF16)
    rest = x - h.astype(F32)
    m = rest.astype(BF16)
    l = (rest - m.astype(F32)).astype(BF16)
    return h, m, l


def nt(a, b):
    return lax.dot_general(a, b, (((1,), (1,)), ((), ())), preferred_element_type=F32)


def gram_kernel(first, last, merge, base, *refs):
    own, r1, r3, r2, factor_ref = refs[:5]
    refs = refs[5:]
    acc_in = None
    if not first:
        acc_in, core_in = refs[:2]
        refs = refs[2:]
    if last:
        mine_ref, give_ref, core_ref, h_scr, m_scr, l_scr, core_scr, acc_ref = refs
    else:
        acc_ref, core_ref, h_scr, m_scr, l_scr, core_scr = refs
    me = lax.axis_index("narrow")
    step = pl.program_id(0)
    for shift, piece in ((0, own), (1, r1), (3, r3), (2, r2)):
        row = pl.multiple_of(lax.rem(me + 4 - shift, 4) * 128, 128)
        for a in range(4):
            h, m, l = split(piece[a])
            lanes = slice(a * 128, (a + 1) * 128)
            h_scr[pl.ds(row, 128), lanes] = h
            m_scr[pl.ds(row, 128), lanes] = m
            l_scr[pl.ds(row, 128), lanes] = l

    @pl.when(step == 0)
    def _():
        if first:
            acc_ref[...] = jnp.zeros_like(acc_ref)
        else:
            acc_ref[...] = acc_in[...]
        if merge:
            core_scr[:, :64] = core_in[...]

    for top, side in ((256, 0), (512, 256)):
        a = [s[:top, :] for s in (h_scr, m_scr, l_scr)]
        b = [s[side:side + 256, :] for s in (h_scr, m_scr, l_scr)]
        part = nt(a[1], b[1])
        part += nt(a[0], b[2])
        part += nt(a[2], b[0])
        part += nt(a[0], b[1])
        part += nt(a[1], b[0])
        part += nt(a[0], b[0])
        for k, (i, j) in enumerate(BLOCKS):
            if side <= j * 128 < side + 256:
                acc_ref[k * 128:(k + 1) * 128, :] += part[
                    i * 128:(i + 1) * 128, j * 128 - side:j * 128 - side + 128
                ]
    f = jnp.concatenate(split(factor_ref[...]), axis=0)
    by_h = jnp.dot(f, h_scr[...], preferred_element_type=F32)
    by_m = jnp.dot(f[:128], m_scr[...], preferred_element_type=F32)
    by_l = jnp.dot(f[:64], l_scr[...], preferred_element_type=F32)
    core = (by_h[128:] + by_l + by_m[64:]) + (by_h[64:128] + by_m[:64]) + by_h[:64]
    for a in range(4):
        part = core[:, a * 128:(a + 1) * 128]
        at = base + 4 * step + a
        core_scr[pl.ds(at, 64, stride=16), :] = part
        core_scr[pl.ds(at + 8, 64, stride=16), :] = pltpu.roll(part, 64, 1)

    @pl.when(step == pl.num_programs(0) - 1)
    def _():
        core_ref[...] = core_scr[:, :64]
        if last:
            c = lax.axis_index("core")
            mine_ref[...] = acc_ref[pl.ds(pl.multiple_of(c * HALF, 128), HALF), :]
            give_ref[...] = acc_ref[pl.ds(pl.multiple_of((1 - c) * HALF, 128), HALF), :]


def gram_step(comp, base, pieces, factor_t, acc, core, last):
    first = acc is None
    merge = base > 0
    depth = pieces[0].shape[0]
    piece_spec = pl.BlockSpec((4, 128, 128), lambda s: (s, 0, 0))
    whole = lambda s: (0, 0)
    in_specs = [piece_spec] * 4 + [pl.BlockSpec((64, 512), whole)]
    core_spec = pl.BlockSpec((None, 1024, 64), lambda s: (comp, 0, 0))
    args = list(pieces) + [factor_t]
    aliases = {}
    if not first:
        in_specs += [
            pl.BlockSpec((1280, 128), whole),
            core_spec if merge else pl.BlockSpec(memory_space=pl.ANY),
        ]
        args += [acc, core]
        aliases = {6: 2} if last else {5: 0, 6: 1}
    sums = [HALF, HALF] if last else [1280]
    scratch = [pltpu.VMEM((512, 512), BF16)] * 3 + [pltpu.VMEM((1024, 128), F32)]
    if last:
        scratch.append(pltpu.VMEM((1280, 128), F32))
    return pl.pallas_call(
        functools.partial(gram_kernel, first, last, merge, base),
        grid=(depth // 4,),
        in_specs=in_specs,
        out_specs=[pl.BlockSpec((r, 128), whole) for r in sums] + [core_spec],
        out_shape=[jax.ShapeDtypeStruct((r, 128), F32) for r in sums]
        + [jax.ShapeDtypeStruct((4, 1024, 64), F32)],
        scratch_shapes=scratch,
        input_output_aliases=aliases,
        compiler_params=pltpu.CompilerParams(vmem_limit_bytes=40 << 20),
        cost_estimate=pl.CostEstimate(
            flops=(6 << 26) * depth, bytes_accessed=depth << 19, transcendentals=0
        ),
        name="gram",
    )(*args)


def total(mine, give):
    swap = [(0, 1), (1, 0)]
    plane = lax.axis_size("z") * lax.axis_size("y")
    h = mine + lax.ppermute(give, "core", swap)
    h = h.reshape(plane, HALF // plane, 128)
    deal = lambda x, axes: lax.all_to_all(x, axes, 0, 0, tiled=True)
    spread = lambda x, n: jnp.broadcast_to(x[None], (n,) + x.shape)
    piece = jnp.sum(deal(h, ("z", "y")), axis=0)
    piece = jnp.sum(deal(spread(piece, lax.axis_size("narrow")), "narrow"), axis=0)
    h = deal(spread(piece, plane), ("z", "y")).reshape(HALF, 128)
    return h, lax.ppermute(h, "core", swap)


def factor_block(work, out_ref, b, tiles):
    lane = lax.broadcasted_iota(jnp.int32, (8, 128), 1)
    sub = lax.broadcasted_iota(jnp.int32, (8, 128), 0)
    base = b * 128
    spread = lambda v, i: jnp.broadcast_to(v[i:i + 1, :], (8, 128))
    column = lambda v, j: jnp.broadcast_to(v[:, j:j + 1], (8, 128))
    for p in range(16):
        at = base + 8 * p
        head = work[b, at:at + 8, :]
        cols = [column(head, 8 * p + j) for j in range(8)]
        c = {(i, j): spread(cols[j], i) for j in range(8) for i in range(j + 1)}
        rs, u = [], {}
        for k in range(8):
            r = lax.rsqrt(c[k, k])
            rs.append(r)
            for j in range(k + 1, 8):
                u[k, j] = c[k, j] * r
            for j in range(k + 1, 8):
                for i in range(k + 1, j + 1):
                    c[i, j] = c[i, j] - u[k, i] * u[k, j]
        rows = {}
        for t in tiles:
            x = head if t == b else work[t, at:at + 8, :]
            made = []
            for k in range(8):
                v = spread(x, k)
                for m in range(k):
                    v = v - u[m, k] * made[m]
                made.append(v * rs[k])
            rows[t] = made
            full = made[0]
            for k in range(1, 8):
                full = jnp.where(sub >= k, made[k], full)
            if t == b:
                full = jnp.where(lane >= sub + 8 * p, full, 0.0)
            out_ref[at:at + 8, t * 128:(t + 1) * 128] = full
        for g in range(p + 1, 16):
            ag = base + 8 * g
            a = work[b, ag:ag + 8, :]
            left = [column(a, 8 * p + j) for j in range(8)]
            ug = []
            for k in range(8):
                w = left[k] * rs[k]
                ug.append(w)
                for j in range(k + 1, 8):
                    left[j] = left[j] - w * u[k, j]
            for t in tiles:
                v = a if t == b else work[t, ag:ag + 8, :]
                for k in range(8):
                    v = v - ug[k] * rows[t][k]
                work[t, ag:ag + 8, :] = v


def chol_kernel(scale, mine_ref, other_ref, out_ref, gram, work):
    c = lax.axis_index("core")
    gram[pl.ds(pl.multiple_of(c * HALF, 128), HALF), :] = mine_ref[...]
    gram[pl.ds(pl.multiple_of((1 - c) * HALF, 128), HALF), :] = other_ref[...]
    for k, (i, j) in enumerate(BLOCKS):
        work[j, i * 128:(i + 1) * 128, :] = gram[k * 128:(k + 1) * 128, :] * scale
    for b in range(4):
        factor_block(work, out_ref, b, range(b, 4))
        for t in range(b):
            out_ref[b * 128:(b + 1) * 128, t * 128:(t + 1) * 128] = jnp.zeros((128, 128), F32)
        if b < 3:
            tail = out_ref[b * 128:(b + 1) * 128, (b + 1) * 128:]
            for i in range(b + 1, 4):
                o = (i - b - 1) * 128
                part = lax.dot_general(
                    tail[:, o:o + 128],
                    tail[:, o:],
                    (((0,), (0,)), ((), ())),
                    precision=HI,
                    preferred_element_type=F32,
                )
                for j in range(i, 4):
                    work[j, i * 128:(i + 1) * 128, :] -= part[:, (j - i) * 128:(j - i + 1) * 128]


def upper_factor(mine, other, scale):
    return pl.pallas_call(
        functools.partial(chol_kernel, scale),
        out_shape=jax.ShapeDtypeStruct((512, 512), F32),
        in_specs=[pl.BlockSpec((HALF, 128), lambda: (0, 0))] * 2,
        out_specs=pl.BlockSpec((512, 512), lambda: (0, 0)),
        scratch_shapes=[pltpu.VMEM((1280, 128), F32), pltpu.VMEM((4, 512, 128), F32)],
        name="upper_factor",
    )(mine, other)


def on_device(slab, factor):
    count, own, second, third = slab.shape
    ncol_total = count * second * lax.axis_size(WIDE) * third
    flat = slab.reshape(count, own * second, third)
    factor_t = factor.T
    acc = core = None
    chunks = []
    for c in range(count):
        parts = 2 if c == count - 1 else 1
        for k, p in enumerate(pack(flat, c, parts)):
            chunks.append((c, k * (8 // parts), p))
    for at, (c, base, p) in enumerate(chunks):
        got = [lax.ppermute(p[k], "narrow", ring(4, k)) for k in SHIFTS]
        last = at == len(chunks) - 1
        made = gram_step(c, base, [p[0]] + got, factor_t, acc, core, last)
        if last:
            mine, give, core = made
        else:
            acc, core = made
    mine, other = total(mine, give)
    r_factor = upper_factor(mine, other, 1.0 / ncol_total)
    return (r_factor, core.reshape(count, 64, second, 64))


def solution(mesh):
    narrow = mesh.shape["narrow"]
    fine = Mesh(mesh.devices.reshape(4, 4, 2, narrow), WIDE + ("narrow",))
    return jax.shard_map(
        on_device,
        mesh=fine,
        in_specs=(P(None, "narrow", WIDE, None), P()),
        out_specs=(P(), P(None, None, WIDE, "narrow")),
        check_vma=False,
    )
```

profile of v0, /device:TPU:1, one launch (start us, length us, event | category | flops | bytes accessed | tf_op | source)
XLA Modules:
  0.0 169.9 jit_solution(10985742812183916257)
XLA Ops:
  0.6 4.1 %pack.7 = (f32[8,128,128]{2,1,0:T(8,128)}, f32[8,128,128]{2,1,0:T(8,128)}, f32[8,128,128]{2,1,0:T(8,128)}, f32[8,128,128]{2,1,0:T(8,128)}) custom-call(f32[4,2048,256]{2,1,0:T(8,128)} %bitcast.10, f32[4,2048,256]{2,1,0:T(8,128)} %bitcast.11), custom_call_target="tpu_custom_call" | custom-call | flops 1048576 | bytes 4194304 | tf_op jit(solution)/shard_map/pack/pallas_call | solution.py:50
  4.7 2.0 %collective-permute-start.12 = (f32[8,128,128]{2,1,0:T(8,128)}, f32[8,128,128]{2,1,0:T(8,128)S(1)}, u32[]{:S(2)}, u32[]{:S(2)}) collective-permute-start(f32[8,128,128]{2,1,0:T(8,128)} %get-tuple-element.50), channel_id=1, source_target_pairs={{0,1},{1,2},{2,3},{3,0},{4,5},{5,6},{6,7},{7,4},{8,9},{9,10},{10,1... | collective-permute-start | bytes 1572872 | tf_op jit(solution)/shard_map/ppermute | solution.py:296
  9.7 4.1 %pack.6 = (f32[8,128,128]{2,1,0:T(8,128)}, f32[8,128,128]{2,1,0:T(8,128)}, f32[8,128,128]{2,1,0:T(8,128)}, f32[8,128,128]{2,1,0:T(8,128)}) custom-call(f32[4,2048,256]{2,1,0:T(8,128)} %bitcast.12, f32[4,2048,256]{2,1,0:T(8,128)} %bitcast.13), custom_call_target="tpu_custom_call" | custom-call | flops 1048576 | bytes 4194304 | tf_op jit(solution)/shard_map/pack/pallas_call | solution.py:50
  15.9 3.5 %collective-permute-done.12.refs_1_ = f32[8,128,128]{2,1,0:T(8,128)S(1)} collective-permute-done((f32[8,128,128]{2,1,0:T(8,128)}, f32[8,128,128]{2,1,0:T(8,128)S(1)}, u32[]{:S(2)}, u32[]{:S(2)}) %collective-permute-start.12) | collective-permute-done | bytes 524320 | tf_op jit(solution)/shard_map/ppermute | solution.py:296
  19.7 4.1 %pack.5 = (f32[8,128,128]{2,1,0:T(8,128)}, f32[8,128,128]{2,1,0:T(8,128)}, f32[8,128,128]{2,1,0:T(8,128)}, f32[8,128,128]{2,1,0:T(8,128)}) custom-call(f32[4,2048,256]{2,1,0:T(8,128)} %bitcast.14, f32[4,2048,256]{2,1,0:T(8,128)} %bitcast.15), custom_call_target="tpu_custom_call" | custom-call | flops 1048576 | bytes 4194304 | tf_op jit(solution)/shard_map/pack/pallas_call | solution.py:50
  23.8 4.3 %pack.4 = (f32[4,128,128]{2,1,0:T(8,128)}, f32[4,128,128]{2,1,0:T(8,128)}, f32[4,128,128]{2,1,0:T(8,128)}, f32[4,128,128]{2,1,0:T(8,128)}, f32[4,128,128]{2,1,0:...) custom-call(f32[4,2048,256]{2,1,0:T(8,128)} %bitcast.16, f32[4,2048,256]{2,1,0:T(8,128)} %bitcast.17), custom_call_target="tpu_custom_call" | custom-call | flops 1048576 | bytes 4194304 | tf_op jit(solution)/shard_map/pack/pallas_call | solution.py:50
  29.4 2.7 %collective-permute-done.14.refs_3_ = f32[8,128,128]{2,1,0:T(8,128)} collective-permute-done((f32[8,128,128]{2,1,0:T(8,128)}, f32[8,128,128]{2,1,0:T(8,128)}, u32[]{:S(2)}, u32[]{:S(2)}) %collective-permute-start.14) | collective-permute-done | bytes 524320 | tf_op jit(solution)/shard_map/ppermute | solution.py:296
  33.2 8.7 %collective-permute-done.10.refs_2_ = f32[8,128,128]{2,1,0:T(8,128)S(1)} collective-permute-done((f32[8,128,128]{2,1,0:T(8,128)}, f32[8,128,128]{2,1,0:T(8,128)S(1)}, u32[]{:S(2)}, u32[]{:S(2)}) %collective-permute-start.10) | collective-permute-done | bytes 524320 | tf_op jit(solution)/shard_map/ppermute | solution.py:296
  41.9 2.4 %collective-permute-start.8 = (f32[8,128,128]{2,1,0:T(8,128)}, f32[8,128,128]{2,1,0:T(8,128)S(1)}, u32[]{:S(2)}, u32[]{:S(2)}) collective-permute-start(f32[8,128,128]{2,1,0:T(8,128)} %get-tuple-element.44), channel_id=1, source_target_pairs={{0,2},{1,3},{2,0},{3,1},{4,6},{5,7},{6,4},{7,5},{8,10},{9,11},{10,... | collective-permute-start | bytes 1572872 | tf_op jit(solution)/shard_map/ppermute | solution.py:296
  44.4 6.0 %gram.5 = (f32[1280,128]{1,0:T(8,128)S(1)}, f32[4,1024,64]{2,1,0:T(8,128)}) custom-call(f32[8,128,128]{2,1,0:T(8,128)S(1)} %copy-done.2, f32[8,128,128]{2,1,0:T(8,128)S(1)} %collective-permute-done.12.refs_1_, f32[8,128,128]{2,1,0:T(8,128)S(1)} %collective-permute-done.13.refs_2_, f32[8,128,128]{2,1,0:T(8,128)} %collective-permute-done.14.refs_3_, ...), custom_call_target="tpu_custom_call" | custom-call | flops 3221225472 | bytes 4194304 | tf_op jit(solution)/shard_map/gram/pallas_call | solution.py:165
  50.4 4.6 %collective-permute-start.3 = (f32[4,128,128]{2,1,0:T(8,128)S(1)}, f32[4,128,128]{2,1,0:T(8,128)S(1)}, u32[]{:S(2)}, u32[]{:S(2)}) collective-permute-start(f32[4,128,128]{2,1,0:T(8,128)S(1)} %copy-done.13), channel_id=1, source_target_pairs={{0,1},{1,2},{2,3},{3,0},{4,5},{5,6},{6,7},{7,4},{8,9},{9,10},{10,1... | collective-permute-start | bytes 786440 | tf_op jit(solution)/shard_map/ppermute | solution.py:296
  55.7 5.0 %gram.6 = (f32[1280,128]{1,0:T(8,128)S(1)}, f32[4,1024,64]{2,1,0:T(8,128)}) custom-call(f32[8,128,128]{2,1,0:T(8,128)S(1)} %copy-done.1, f32[8,128,128]{2,1,0:T(8,128)S(1)} %collective-permute-done.9.refs_1_, f32[8,128,128]{2,1,0:T(8,128)S(1)} %collective-permute-done.10.refs_2_, ...), custom_call_target="tpu_custom_call", output_to_operand_aliasing={{0}: (5, {}), {1}: (6, {})} | custom-call | flops 3221225472 | bytes 4194304 | tf_op jit(solution)/shard_map/gram/pallas_call | solution.py:165
  60.8 22.8 %collective-permute-done.3.refs_1_ = f32[4,128,128]{2,1,0:T(8,128)S(1)} collective-permute-done((f32[4,128,128]{2,1,0:T(8,128)S(1)}, f32[4,128,128]{2,1,0:T(8,128)S(1)}, u32[]{:S(2)}, u32[]{:S(2)}) %collective-permute-start.3) | collective-permute-done | bytes 262176 | tf_op jit(solution)/shard_map/ppermute | solution.py:296
  84.1 2.7 %collective-permute-start.1 = (f32[4,128,128]{2,1,0:T(8,128)S(1)}, f32[4,128,128]{2,1,0:T(8,128)S(1)}, u32[]{:S(2)}, u32[]{:S(2)}) collective-permute-start(f32[4,128,128]{2,1,0:T(8,128)S(1)} %copy-done.9), channel_id=1, source_target_pairs={{0,3},{1,0},{2,1},{3,2},{4,7},{5,4},{6,5},{7,6},{8,11},{9,8},{10,9... | collective-permute-start | bytes 786440 | tf_op jit(solution)/shard_map/ppermute | solution.py:296
  88.0 5.0 %gram.7 = (f32[1280,128]{1,0:T(8,128)S(1)}, f32[4,1024,64]{2,1,0:T(8,128)}) custom-call(f32[8,128,128]{2,1,0:T(8,128)S(1)} %copy-done, f32[8,128,128]{2,1,0:T(8,128)S(1)} %collective-permute-done.6.refs_1_, f32[8,128,128]{2,1,0:T(8,128)S(1)} %collective-permute-done.7.refs_2_, ...), custom_call_target="tpu_custom_call", output_to_operand_aliasing={{0}: (5, {}), {1}: (6, {})} | custom-call | flops 3221225472 | bytes 4194304 | tf_op jit(solution)/shard_map/gram/pallas_call | solution.py:165
  93.1 2.9 %gram.8 = (f32[1280,128]{1,0:T(8,128)S(1)}, f32[4,1024,64]{2,1,0:T(8,128)}) custom-call(f32[4,128,128]{2,1,0:T(8,128)S(1)} %copy-done.4, f32[4,128,128]{2,1,0:T(8,128)S(1)} %collective-permute-done.3.refs_1_, f32[4,128,128]{2,1,0:T(8,128)S(1)} %collective-permute-done.4.refs_2_, ...), custom_call_target="tpu_custom_call", output_to_operand_aliasing={{0}: (5, {}), {1}: (6, {})} | custom-call | flops 1610612736 | bytes 2097152 | tf_op jit(solution)/shard_map/gram/pallas_call | solution.py:165
  96.0 3.7 %collective-permute-done.refs_1_ = f32[4,128,128]{2,1,0:T(8,128)S(1)} collective-permute-done((f32[4,128,128]{2,1,0:T(8,128)S(1)}, f32[4,128,128]{2,1,0:T(8,128)S(1)}, u32[]{:S(2)}, u32[]{:S(2)}) %collective-permute-start) | collective-permute-done | bytes 262176 | tf_op jit(solution)/shard_map/ppermute | solution.py:296
  99.7 4.0 %collective-permute-done.2.refs_3_ = f32[4,128,128]{2,1,0:T(8,128)S(1)} collective-permute-done((f32[4,128,128]{2,1,0:T(8,128)S(1)}, f32[4,128,128]{2,1,0:T(8,128)S(1)}, u32[]{:S(2)}, u32[]{:S(2)}) %collective-permute-start.2) | collective-permute-done | bytes 262176 | tf_op jit(solution)/shard_map/ppermute | solution.py:296
  103.7 4.0 %gram.9 = (f32[640,128]{1,0:T(8,128)S(1)}, f32[640,128]{1,0:T(8,128)S(1)}, f32[4,1024,64]{2,1,0:T(8,128)}) custom-call(f32[4,128,128]{2,1,0:T(8,128)S(1)} %copy-done.3, f32[4,128,128]{2,1,0:T(8,128)S(1)} %collective-permute-done.refs_1_, f32[4,128,128]{2,1,0:T(8,128)S(1)} %collective-permute-done.1.refs_2_, ...), custom_call_target="tpu_custom_call", output_to_operand_aliasing={{2}: (6, {})} | custom-call | flops 1610612736 | bytes 2097152 | tf_op jit(solution)/shard_map/gram/pallas_call | solution.py:165
  110.4 16.4 %all_to_all.15 = f32[16,40,128]{2,1,0:T(8,128)S(1)} all-to-all(f32[16,40,128]{2,1,0:T(8,128)S(1)} %bitcast.20), channel_id=1, replica_groups=mesh['z'=4,'y'=4,'core'=2,'narrow'=4] {'z','y'}, dimensions={0} | all-to-all | bytes 655360 | tf_op jit(solution)/shard_map/all_to_all | solution.py:187
  126.8 6.9 %all_to_all.16 = f32[4,40,128]{2,1,0:T(8,128)S(1)} all-to-all(f32[4,40,128]{2,1,0:T(8,128)S(1)} %broadcast_in_dim.4), channel_id=1, replica_groups=mesh['z'=4,'y'=4,'core'=2,'narrow'=4] {'narrow'}, dimensions={0} | all-to-all | bytes 163840 | tf_op jit(solution)/shard_map/all_to_all | solution.py:187
  133.8 10.7 %all_to_all.17 = f32[16,40,128]{2,1,0:T(8,128)S(1)} all-to-all(f32[16,40,128]{2,1,0:T(8,128)S(1)} %broadcast_in_dim.5), channel_id=1, replica_groups=mesh['z'=4,'y'=4,'core'=2,'narrow'=4] {'z','y'}, dimensions={0} | all-to-all | bytes 655360 | tf_op jit(solution)/shard_map/all_to_all | solution.py:187
  144.5 3.9 %collective-permute-start.16 = (f32[640,128]{1,0:T(8,128)S(1)}, f32[640,128]{1,0:T(8,128)S(1)}, u32[]{:S(2)}, u32[]{:S(2)}) collective-permute-start(f32[640,128]{1,0:T(8,128)S(1)} %bitcast.18), channel_id=1, source_target_pairs={{0,4},{4,0},{1,5},{5,1},{2,6},{6,2},{3,7},{7,3},{8,12},{12,8},{9,1... | collective-permute-start | bytes 983048 | tf_op jit(solution)/shard_map/ppermute | solution.py:192
  150.4 19.5 %upper_factor.1 = f32[512,512]{1,0:T(8,128)} custom-call(f32[640,128]{1,0:T(8,128)} %bitcast.19, f32[640,128]{1,0:T(8,128)} %copy-done.7), custom_call_target="tpu_custom_call" | custom-call | tf_op jit(solution)/shard_map/upper_factor/pallas_call | solution.py:274
  (56 shorter events, 15.0 us)
Async XLA Ops:
  4.7 14.7 %collective-permute-start.12 = (f32[8,128,128]{2,1,0:T(8,128)}, f32[8,128,128]{2,1,0:T(8,128)S(1)}, u32[]{:S(2)}, u32[]{:S(2)}) collective-permute-start(f32[8,128,128]{2,1,0:T(8,128)} %get-tuple-element.50), channel_id=1, source_target_pairs={{0,1},{1,2},{2,3},{3,0},{4,5},{5,6},{6,7},{7,4},{8,9},{9,10},{10,1... | collective-permute-start | bytes 1572872 | tf_op jit(solution)/shard_map/ppermute | solution.py:296
  6.7 21.4 %collective-permute-start.13 = (f32[8,128,128]{2,1,0:T(8,128)}, f32[8,128,128]{2,1,0:T(8,128)S(1)}, u32[]{:S(2)}, u32[]{:S(2)}) collective-permute-start(f32[8,128,128]{2,1,0:T(8,128)} %get-tuple-element.51), channel_id=1, source_target_pairs={{0,3},{1,0},{2,1},{3,2},{4,7},{5,4},{6,5},{7,6},{8,11},{9,8},{10,9... | collective-permute-start | bytes 1572872 | tf_op jit(solution)/shard_map/ppermute | solution.py:296
  8.1 24.0 %collective-permute-start.14 = (f32[8,128,128]{2,1,0:T(8,128)}, f32[8,128,128]{2,1,0:T(8,128)}, u32[]{:S(2)}, u32[]{:S(2)}) collective-permute-start(f32[8,128,128]{2,1,0:T(8,128)} %get-tuple-element.52), channel_id=1, source_target_pairs={{0,2},{1,3},{2,0},{3,1},{4,6},{5,7},{6,4},{7,5},{8,10},{9,11},{10,... | collective-permute-start | bytes 1572872 | tf_op jit(solution)/shard_map/ppermute | solution.py:296
  13.8 28.2 %collective-permute-start.10 = (f32[8,128,128]{2,1,0:T(8,128)}, f32[8,128,128]{2,1,0:T(8,128)S(1)}, u32[]{:S(2)}, u32[]{:S(2)}) collective-permute-start(f32[8,128,128]{2,1,0:T(8,128)} %get-tuple-element.47), channel_id=1, source_target_pairs={{0,3},{1,0},{2,1},{3,2},{4,7},{5,4},{6,5},{7,6},{8,11},{9,8},{10,9... | collective-permute-start | bytes 1572872 | tf_op jit(solution)/shard_map/ppermute | solution.py:296
  14.6 35.8 %collective-permute-start.11 = (f32[8,128,128]{2,1,0:T(8,128)}, f32[8,128,128]{2,1,0:T(8,128)S(1)}, u32[]{:S(2)}, u32[]{:S(2)}) collective-permute-start(f32[8,128,128]{2,1,0:T(8,128)} %get-tuple-element.48), channel_id=1, source_target_pairs={{0,2},{1,3},{2,0},{3,1},{4,6},{5,7},{6,4},{7,5},{8,10},{9,11},{10,... | collective-permute-start | bytes 1572872 | tf_op jit(solution)/shard_map/ppermute | solution.py:296
  19.4 36.1 %collective-permute-start.9 = (f32[8,128,128]{2,1,0:T(8,128)}, f32[8,128,128]{2,1,0:T(8,128)S(1)}, u32[]{:S(2)}, u32[]{:S(2)}) collective-permute-start(f32[8,128,128]{2,1,0:T(8,128)} %get-tuple-element.46), channel_id=1, source_target_pairs={{0,1},{1,2},{2,3},{3,0},{4,5},{5,6},{6,7},{7,4},{8,9},{9,10},{10,1... | collective-permute-start | bytes 1572872 | tf_op jit(solution)/shard_map/ppermute | solution.py:296
  23.8 20.6 %copy-start.2 = (f32[8,128,128]{2,1,0:T(8,128)S(1)}, f32[8,128,128]{2,1,0:T(8,128)}, u32[]{:S(2)}) copy-start(f32[8,128,128]{2,1,0:T(8,128)} %get-tuple-element.49.refs_0_) | copy-start | bytes 1572868
  23.8 20.6 %copy-start.5 = (f32[512,64]{0,1:T(8,128)S(1)}, f32[512,64]{0,1:T(8,128)}, u32[]{:S(2)}) copy-start(f32[512,64]{0,1:T(8,128)} %param.3) | copy-start | bytes 393220
  28.1 55.9 %collective-permute-start.6 = (f32[8,128,128]{2,1,0:T(8,128)}, f32[8,128,128]{2,1,0:T(8,128)S(1)}, u32[]{:S(2)}, u32[]{:S(2)}) collective-permute-start(f32[8,128,128]{2,1,0:T(8,128)} %get-tuple-element.42), channel_id=1, source_target_pairs={{0,1},{1,2},{2,3},{3,0},{4,5},{5,6},{6,7},{7,4},{8,9},{9,10},{10,1... | collective-permute-start | bytes 1572872 | tf_op jit(solution)/shard_map/ppermute | solution.py:296
  32.1 51.9 %collective-permute-start.7 = (f32[8,128,128]{2,1,0:T(8,128)}, f32[8,128,128]{2,1,0:T(8,128)S(1)}, u32[]{:S(2)}, u32[]{:S(2)}) collective-permute-start(f32[8,128,128]{2,1,0:T(8,128)} %get-tuple-element.43), channel_id=1, source_target_pairs={{0,3},{1,0},{2,1},{3,2},{4,7},{5,4},{6,5},{7,6},{8,11},{9,8},{10,9... | collective-permute-start | bytes 1572872 | tf_op jit(solution)/shard_map/ppermute | solution.py:296
  41.9 44.8 %collective-permute-start.8 = (f32[8,128,128]{2,1,0:T(8,128)}, f32[8,128,128]{2,1,0:T(8,128)S(1)}, u32[]{:S(2)}, u32[]{:S(2)}) collective-permute-start(f32[8,128,128]{2,1,0:T(8,128)} %get-tuple-element.44), channel_id=1, source_target_pairs={{0,2},{1,3},{2,0},{3,1},{4,6},{5,7},{6,4},{7,5},{8,10},{9,11},{10,... | collective-permute-start | bytes 1572872 | tf_op jit(solution)/shard_map/ppermute | solution.py:296
  50.4 33.1 %collective-permute-start.3 = (f32[4,128,128]{2,1,0:T(8,128)S(1)}, f32[4,128,128]{2,1,0:T(8,128)S(1)}, u32[]{:S(2)}, u32[]{:S(2)}) collective-permute-start(f32[4,128,128]{2,1,0:T(8,128)S(1)} %copy-done.13), channel_id=1, source_target_pairs={{0,1},{1,2},{2,3},{3,0},{4,5},{5,6},{6,7},{7,4},{8,9},{9,10},{10,1... | collective-permute-start | bytes 786440 | tf_op jit(solution)/shard_map/ppermute | solution.py:296
  55.5 37.6 %collective-permute-start.4 = (f32[4,128,128]{2,1,0:T(8,128)S(1)}, f32[4,128,128]{2,1,0:T(8,128)S(1)}, u32[]{:S(2)}, u32[]{:S(2)}) collective-permute-start(f32[4,128,128]{2,1,0:T(8,128)S(1)} %copy-done.12), channel_id=1, source_target_pairs={{0,3},{1,0},{2,1},{3,2},{4,7},{5,4},{6,5},{7,6},{8,11},{9,8},{10,9... | collective-permute-start | bytes 786440 | tf_op jit(solution)/shard_map/ppermute | solution.py:296
  55.7 27.9 %copy-start.11 = (f32[4,128,128]{2,1,0:T(8,128)S(1)}, f32[4,128,128]{2,1,0:T(8,128)}, u32[]{:S(2)}) copy-start(f32[4,128,128]{2,1,0:T(8,128)} %get-tuple-element.40) | copy-start | bytes 786436
  55.7 28.3 %copy-start.10 = (f32[4,128,128]{2,1,0:T(8,128)S(1)}, f32[4,128,128]{2,1,0:T(8,128)}, u32[]{:S(2)}) copy-start(f32[4,128,128]{2,1,0:T(8,128)} %get-tuple-element.34) | copy-start | bytes 786436
  55.7 28.3 %copy-start.9 = (f32[4,128,128]{2,1,0:T(8,128)S(1)}, f32[4,128,128]{2,1,0:T(8,128)}, u32[]{:S(2)}) copy-start(f32[4,128,128]{2,1,0:T(8,128)} %get-tuple-element.35) | copy-start | bytes 786436
  55.7 31.0 %copy-start.8 = (f32[4,128,128]{2,1,0:T(8,128)S(1)}, f32[4,128,128]{2,1,0:T(8,128)}, u32[]{:S(2)}) copy-start(f32[4,128,128]{2,1,0:T(8,128)} %get-tuple-element.36) | copy-start | bytes 786436
  55.7 32.3 %copy-start = (f32[8,128,128]{2,1,0:T(8,128)S(1)}, f32[8,128,128]{2,1,0:T(8,128)}, u32[]{:S(2)}) copy-start(f32[8,128,128]{2,1,0:T(8,128)} %get-tuple-element.41.refs_0_) | copy-start | bytes 1572868
  83.6 9.5 %collective-permute-start.5 = (f32[4,128,128]{2,1,0:T(8,128)S(1)}, f32[4,128,128]{2,1,0:T(8,128)S(1)}, u32[]{:S(2)}, u32[]{:S(2)}) collective-permute-start(f32[4,128,128]{2,1,0:T(8,128)S(1)} %copy-done.11), channel_id=1, source_target_pairs={{0,2},{1,3},{2,0},{3,1},{4,6},{5,7},{6,4},{7,5},{8,10},{9,11},{10,... | collective-permute-start | bytes 786440 | tf_op jit(solution)/shard_map/ppermute | solution.py:296
  84.0 15.7 %collective-permute-start = (f32[4,128,128]{2,1,0:T(8,128)S(1)}, f32[4,128,128]{2,1,0:T(8,128)S(1)}, u32[]{:S(2)}, u32[]{:S(2)}) collective-permute-start(f32[4,128,128]{2,1,0:T(8,128)S(1)} %copy-done.10), channel_id=1, source_target_pairs={{0,1},{1,2},{2,3},{3,0},{4,5},{5,6},{6,7},{7,4},{8,9},{9,10},{10,1... | collective-permute-start | bytes 786440 | tf_op jit(solution)/shard_map/ppermute | solution.py:296
  84.1 15.7 %collective-permute-start.1 = (f32[4,128,128]{2,1,0:T(8,128)S(1)}, f32[4,128,128]{2,1,0:T(8,128)S(1)}, u32[]{:S(2)}, u32[]{:S(2)}) collective-permute-start(f32[4,128,128]{2,1,0:T(8,128)S(1)} %copy-done.9), channel_id=1, source_target_pairs={{0,3},{1,0},{2,1},{3,2},{4,7},{5,4},{6,5},{7,6},{8,11},{9,8},{10,9... | collective-permute-start | bytes 786440 | tf_op jit(solution)/shard_map/ppermute | solution.py:296
  86.7 17.0 %collective-permute-start.2 = (f32[4,128,128]{2,1,0:T(8,128)S(1)}, f32[4,128,128]{2,1,0:T(8,128)S(1)}, u32[]{:S(2)}, u32[]{:S(2)}) collective-permute-start(f32[4,128,128]{2,1,0:T(8,128)S(1)} %copy-done.8), channel_id=1, source_target_pairs={{0,2},{1,3},{2,0},{3,1},{4,6},{5,7},{6,4},{7,5},{8,10},{9,11},{10,... | collective-permute-start | bytes 786440 | tf_op jit(solution)/shard_map/ppermute | solution.py:296
  107.8 2.6 %collective-permute-start.15 = (f32[640,128]{1,0:T(8,128)S(1)}, f32[640,128]{1,0:T(8,128)S(1)}, u32[]{:S(2)}, u32[]{:S(2)}) collective-permute-start(f32[640,128]{1,0:T(8,128)S(1)} %get-tuple-element.62), channel_id=1, source_target_pairs={{0,4},{4,0},{1,5},{5,1},{2,6},{6,2},{3,7},{7,3},{8,12},{12,8},{9,1... | collective-permute-start | bytes 983048 | tf_op jit(solution)/shard_map/ppermute | solution.py:185
  144.5 5.1 %collective-permute-start.16 = (f32[640,128]{1,0:T(8,128)S(1)}, f32[640,128]{1,0:T(8,128)S(1)}, u32[]{:S(2)}, u32[]{:S(2)}) collective-permute-start(f32[640,128]{1,0:T(8,128)S(1)} %bitcast.18), channel_id=1, source_target_pairs={{0,4},{4,0},{1,5},{5,1},{2,6},{6,2},{3,7},{7,3},{8,12},{12,8},{9,1... | collective-permute-start | bytes 983048 | tf_op jit(solution)/shard_map/ppermute | solution.py:192
  (7 other events, 50.0 us)
where the time goes:
time: 170 us
  Pallas kernels  59 us (35%)
  waiting for transfers between devices  48.4 us (28%)
  blocking collectives  34 us (20%)
  starting transfers between devices  26.8 us (16%)
    ppermute x15, waiting for transfers between devices, on_device(): got = [lax.ppermute(p[k], 'narrow', ring(4, k)) for k in SHIFTS]  45.9 us
    all_to_all x3, blocking collectives, total(): deal = lambda x, axes: lax.all_to_all(x, axes, 0, 0, tiled=True)  34 us
    pallas_call x5, Pallas kernels, gram_step(): pl.pallas_call(functools.partial(gram_kernel, first, last, merge, base),...  23 us
    ppermute x15, starting transfers between devices, on_device(): got = [lax.ppermute(p[k], 'narrow', ring(4, k)) for k in SHIFTS]  21.6 us
    pallas_call x1, Pallas kernels, upper_factor(): pl.pallas_call(functools.partial(chol_kernel, scale), out_shape=jax.Shape...  19.5 us
    pallas_call x4, Pallas kernels, pack(): pl.pallas_call(pack_kernel, grid=(2,), in_specs=[pl.BlockSpec((None, rows...  16.5 us
    ppermute x1, starting transfers between devices, total(): return (h, lax.ppermute(h, 'core', swap))  3.88 us
  transfers between devices with their start and end apart: 17, of which 9 were waited for; matrix products, arithmetic and copies ran while one was open for 0% of the time, Pallas kernels for 18%

commit v1 on v0

--- a/solution.py
+++ b/solution.py
@@ -9,8 +9,12 @@
 HI = lax.Precision.HIGHEST
 BLOCKS = [(i, j) for i in range(4) for j in range(i, 4)]
 SHIFTS = (1, 3, 2)
+FULL = [(0, 8)]
+HALVES = [(0, 4), (4, 4)]
+PLAN = [(0, FULL), (1, FULL), (2, FULL), (3, HALVES)]
 HALF = 640
 WIDE = ("z", "y", "core")
+PANEL = 8
 F32 = jnp.float32
 BF16 = jnp.bfloat16
 
@@ -19,19 +23,17 @@
     return [(i, (i + shift) % size) for i in range(size)]
 
 
-def pack_kernel(x0_ref, x1_ref, *outs):
+def pack_kernel(ranges, x0_ref, x1_ref, *outs):
     n = lax.axis_index("narrow")
     rows = x0_ref.shape[0] // 16
-    parts = len(outs) // 4
-    depth = 8 // parts
     low = lax.broadcasted_iota(jnp.int32, (rows, 128), 1) < 64
 
     def body(k):
-        for part in range(parts):
+        for part, (base, depth) in enumerate(ranges):
 
             @pl.loop(0, depth)
             def _(a):
-                at = part * depth + a
+                at = base + a
                 for tile, x_ref in enumerate((x0_ref, x1_ref)):
                     lo = x_ref[pl.ds(at, rows, stride=16), :]
                     hi = x_ref[pl.ds(at + 8, rows, stride=16), :]
@@ -44,24 +46,26 @@
         pl.when(n == k)(functools.partial(body, k))
 
 
-def pack(slab, comp, parts):
+def pack(slab, comp, ranges):
     rows = 1024
-    depth = 8 // parts
+    shapes = [(d, 128, 128) for _, d in ranges for _ in range(4)]
     outs = pl.pallas_call(
-        pack_kernel,
+        functools.partial(pack_kernel, ranges),
         grid=(2,),
         in_specs=[
             pl.BlockSpec((None, rows, 128), lambda i: (comp, i, 0)),
             pl.BlockSpec((None, rows, 128), lambda i: (comp, i, 1)),
         ],
-        out_specs=[pl.BlockSpec((depth, rows // 16, 128), lambda i: (0, i, 0))] * (4 * parts),
-        out_shape=[jax.ShapeDtypeStruct((depth, 128, 128), F32)] * (4 * parts),
+        out_specs=[
+            pl.BlockSpec((d, rows // 16, 128), lambda i: (0, i, 0)) for d, _, _ in shapes
+        ],
+        out_shape=[jax.ShapeDtypeStruct(shape, F32) for shape in shapes],
         cost_estimate=pl.CostEstimate(
             flops=1 << 20, bytes_accessed=4 << 20, transcendentals=0
         ),
         name="pack",
     )(slab, slab)
-    return [outs[4 * k:4 * k + 4] for k in range(parts)]
+    return [outs[4 * k:4 * k + 4] for k in range(len(ranges))]
 
 
 def split(x):
@@ -91,7 +95,7 @@
     step = pl.program_id(0)
     for shift, piece in ((0, own), (1, r1), (3, r3), (2, r2)):
         row = pl.multiple_of(lax.rem(me + 4 - shift, 4) * 128, 128)
-        for a in range(4):
+        for a in range(own.shape[0]):
             h, m, l = split(piece[a])
             lanes = slice(a * 128, (a + 1) * 128)
             h_scr[pl.ds(row, 128), lanes] = h
@@ -126,9 +130,10 @@
     by_m = jnp.dot(f[:128], m_scr[...], preferred_element_type=F32)
     by_l = jnp.dot(f[:64], l_scr[...], preferred_element_type=F32)
     core = (by_h[128:] + by_l + by_m[64:]) + (by_h[64:128] + by_m[:64]) + by_h[:64]
-    for a in range(4):
+    depth = own.shape[0]
+    for a in range(depth):
         part = core[:, a * 128:(a + 1) * 128]
-        at = base + 4 * step + a
+        at = base + depth * step + a
         core_scr[pl.ds(at, 64, stride=16), :] = part
         core_scr[pl.ds(at + 8, 64, stride=16), :] = pltpu.roll(part, 64, 1)
 
@@ -145,7 +150,8 @@
     first = acc is None
     merge = base > 0
     depth = pieces[0].shape[0]
-    piece_spec = pl.BlockSpec((4, 128, 128), lambda s: (s, 0, 0))
+    take = min(depth, 4)
+    piece_spec = pl.BlockSpec((take, 128, 128), lambda s: (s, 0, 0))
     whole = lambda s: (0, 0)
     in_specs = [piece_spec] * 4 + [pl.BlockSpec((64, 512), whole)]
     core_spec = pl.BlockSpec((None, 1024, 64), lambda s: (comp, 0, 0))
@@ -159,12 +165,12 @@
         args += [acc, core]
         aliases = {6: 2} if last else {5: 0, 6: 1}
     sums = [HALF, HALF] if last else [1280]
-    scratch = [pltpu.VMEM((512, 512), BF16)] * 3 + [pltpu.VMEM((1024, 128), F32)]
+    scratch = [pltpu.VMEM((512, 128 * take), BF16)] * 3 + [pltpu.VMEM((1024, 128), F32)]
     if last:
         scratch.append(pltpu.VMEM((1280, 128), F32))
     return pl.pallas_call(
         functools.partial(gram_kernel, first, last, merge, base),
-        grid=(depth // 4,),
+        grid=(depth // take,),
         in_specs=in_specs,
         out_specs=[pl.BlockSpec((r, 128), whole) for r in sums] + [core_spec],
         out_shape=[jax.ShapeDtypeStruct((r, 128), F32) for r in sums]
@@ -187,7 +193,8 @@
     deal = lambda x, axes: lax.all_to_all(x, axes, 0, 0, tiled=True)
     spread = lambda x, n: jnp.broadcast_to(x[None], (n,) + x.shape)
     piece = jnp.sum(deal(h, ("z", "y")), axis=0)
-    piece = jnp.sum(deal(spread(piece, lax.axis_size("narrow")), "narrow"), axis=0)
+    for flip in (1, 3):
+        piece += lax.ppermute(piece, "narrow", [(i, i ^ flip) for i in range(4)])
     h = deal(spread(piece, plane), ("z", "y")).reshape(HALF, 128)
     return h, lax.ppermute(h, "core", swap)
 
@@ -201,7 +208,15 @@
     for p in range(16):
         at = base + 8 * p
         head = work[b, at:at + 8, :]
-        cols = [column(head, 8 * p + j) for j in range(8)]
+        if p % PANEL == 0:
+            cols = [column(head, 8 * p + j) for j in range(8)]
+        else:
+            cols = ncols
+        last = p - p % PANEL + PANEL
+        more = p + 1 < last
+        if more:
+            nxt = work[b, at + 8:at + 16, :]
+            ncols = [column(nxt, 8 * (p + 1) + j) for j in range(8)]
         c = {(i, j): spread(cols[j], i) for j in range(8) for i in range(j + 1)}
         rs, u = [], {}
         for k in range(8):
@@ -228,7 +243,7 @@
             if t == b:
                 full = jnp.where(lane >= sub + 8 * p, full, 0.0)
             out_ref[at:at + 8, t * 128:(t + 1) * 128] = full
-        for g in range(p + 1, 16):
+        for g in range(p + 1, last):
             ag = base + 8 * g
             a = work[b, ag:ag + 8, :]
             left = [column(a, 8 * p + j) for j in range(8)]
@@ -238,11 +253,23 @@
                 ug.append(w)
                 for j in range(k + 1, 8):
                     left[j] = left[j] - w * u[k, j]
+                if more and g == p + 1:
+                    for j in range(8):
+                        ncols[j] = ncols[j] - w * spread(w, j)
             for t in tiles:
                 v = a if t == b else work[t, ag:ag + 8, :]
                 for k in range(8):
                     v = v - ug[k] * rows[t][k]
                 work[t, ag:ag + 8, :] = v
+        if p + 1 == last and last < 16:
+            done = out_ref[at + 8 - 8 * PANEL:at + 8, base:]
+            part = lax.dot_general(
+                done[:, :128], done, (((0,), (0,)), ((), ())),
+                precision=HI, preferred_element_type=F32,
+            )
+            for t in tiles:
+                o = (t - b) * 128
+                work[t, base + 8 * last:base + 128, :] -= part[8 * last:, o:o + 128]
 
 
 def chol_kernel(scale, mine_ref, other_ref, out_ref, gram, work):
@@ -288,14 +315,15 @@
     factor_t = factor.T
     acc = core = None
     chunks = []
-    for c in range(count):
-        parts = 2 if c == count - 1 else 1
-        for k, p in enumerate(pack(flat, c, parts)):
-            chunks.append((c, k * (8 // parts), p))
+    for comp, ranges in PLAN:
+        for (base, _), p in zip(ranges, pack(flat, comp, ranges)):
+            chunks.append((comp, base, p))
+    arrived = []
     for at, (c, base, p) in enumerate(chunks):
-        got = [lax.ppermute(p[k], "narrow", ring(4, k)) for k in SHIFTS]
+        arrived.append([lax.ppermute(p[k], "narrow", ring(4, k)) for k in SHIFTS])
+    for at, (c, base, p) in enumerate(chunks):
         last = at == len(chunks) - 1
-        made = gram_step(c, base, [p[0]] + got, factor_t, acc, core, last)
+        made = gram_step(c, base, [p[0]] + arrived[at], factor_t, acc, core, last)
         if last:
             mine, give, core = made
         else:

time: 170 us -> 166 us (0.976)
  blocking collectives: 34 us -> 27.1 us
  waiting for transfers between devices: 48.4 us -> 55 us
  Pallas kernels: 59 us -> 53.6 us
    all_to_all x3 -> x2, blocking collectives: 34 us -> 27.1 us  [total(): deal = lambda x, axes: lax.all_to_all(x, axes, 0, 0, tiled=True)]
    ppermute x15 -> x17, waiting for transfers between devices: 45.9 us -> 52.5 us  [the longest x15 46 us: on_device(): arrived.append([lax.ppermute(p[k], 'narrow', ring(4, k)) for k in SHIFTS])]
    pallas_call x1, Pallas kernels: 19.5 us -> 14.2 us  [upper_factor(): pl.pallas_call(functools.partial(chol_kernel, scale), out_shape=jax.Shape...]
    ppermute x15 -> x17, starting transfers between devices: 21.6 us -> 21.6 us  [the longest x15 21.6 us: on_device(): arrived.append([lax.ppermute(p[k], 'narrow', ring(4, k)) for k in SHIFTS])]
  transfers between devices with their start and end apart: 17 -> 19, of which waited for: 9 -> 11; matrix products, arithmetic and copies ran while one was open for 0% -> 0% of each run, Pallas kernels for 18% -> 19%
where the time goes in v1:
time: 166 us; the launch traced here: 165 us
  waiting for transfers between devices  55 us (33%)
  Pallas kernels  53.6 us (32%)
  starting transfers between devices  28 us (17%)
  blocking collectives  27.1 us (16%)
    ppermute x15, waiting for transfers between devices, on_device(): arrived.append([lax.ppermute(p[k], 'narrow', ring(4, k)) for k in SHIFTS])  46 us
    all_to_all x2, blocking collectives, total(): deal = lambda x, axes: lax.all_to_all(x, axes, 0, 0, tiled=True)  27.1 us
    pallas_call x5, Pallas kernels, gram_step(): pl.pallas_call(functools.partial(gram_kernel, first, last, merge, base),...  23 us
    ppermute x15, starting transfers between devices, on_device(): arrived.append([lax.ppermute(p[k], 'narrow', ring(4, k)) for k in SHIFTS])  21.6 us
    pallas_call x4, Pallas kernels, pack(): pl.pallas_call(functools.partial(pack_kernel, ranges), grid=(2,), in_spec...  16.4 us
    pallas_call x1, Pallas kernels, upper_factor(): pl.pallas_call(functools.partial(chol_kernel, scale), out_shape=jax.Shape...  14.2 us
    ppermute x2, waiting for transfers between devices, total(): piece += lax.ppermute(piece, 'narrow', [(i, i ^ flip) for i in range(4)])  6.46 us
    ppermute x1, starting transfers between devices, total(): return (h, lax.ppermute(h, 'core', swap))  5.03 us
  transfers between devices with their start and end apart: 19, of which 11 were waited for; matrix products, arithmetic and copies ran while one was open for 0% of the time, Pallas kernels for 19%

profile of v1, /device:TPU:1, one launch (start us, length us, event | category | flops | bytes accessed | tf_op | source)
XLA Modules:
  0.0 165.4 jit_solution(958943620692427756)
XLA Ops:
  0.6 4.1 %pack.7 = (f32[8,128,128]{2,1,0:T(8,128)}, f32[8,128,128]{2,1,0:T(8,128)}, f32[8,128,128]{2,1,0:T(8,128)}, f32[8,128,128]{2,1,0:T(8,128)}) custom-call(f32[4,2048,256]{2,1,0:T(8,128)} %bitcast.10, f32[4,2048,256]{2,1,0:T(8,128)} %bitcast.11), custom_call_target="tpu_custom_call" | custom-call | flops 1048576 | bytes 4194304 | tf_op jit(solution)/shard_map/pack/pallas_call | solution.py:52
  9.7 4.1 %pack.6 = (f32[8,128,128]{2,1,0:T(8,128)}, f32[8,128,128]{2,1,0:T(8,128)}, f32[8,128,128]{2,1,0:T(8,128)}, f32[8,128,128]{2,1,0:T(8,128)}) custom-call(f32[4,2048,256]{2,1,0:T(8,128)} %bitcast.12, f32[4,2048,256]{2,1,0:T(8,128)} %bitcast.13), custom_call_target="tpu_custom_call" | custom-call | flops 1048576 | bytes 4194304 | tf_op jit(solution)/shard_map/pack/pallas_call | solution.py:52
  15.9 3.5 %collective-permute-done.12.refs_1_ = f32[8,128,128]{2,1,0:T(8,128)S(1)} collective-permute-done((f32[8,128,128]{2,1,0:T(8,128)}, f32[8,128,128]{2,1,0:T(8,128)S(1)}, u32[]{:S(2)}, u32[]{:S(2)}) %collective-permute-start.12) | collective-permute-done | bytes 524320 | tf_op jit(solution)/shard_map/ppermute | solution.py:323
  19.7 4.1 %pack.5 = (f32[8,128,128]{2,1,0:T(8,128)}, f32[8,128,128]{2,1,0:T(8,128)}, f32[8,128,128]{2,1,0:T(8,128)}, f32[8,128,128]{2,1,0:T(8,128)}) custom-call(f32[4,2048,256]{2,1,0:T(8,128)} %bitcast.14, f32[4,2048,256]{2,1,0:T(8,128)} %bitcast.15), custom_call_target="tpu_custom_call" | custom-call | flops 1048576 | bytes 4194304 | tf_op jit(solution)/shard_map/pack/pallas_call | solution.py:52
  23.8 4.2 %pack.4 = (f32[4,128,128]{2,1,0:T(8,128)}, f32[4,128,128]{2,1,0:T(8,128)}, f32[4,128,128]{2,1,0:T(8,128)}, f32[4,128,128]{2,1,0:T(8,128)}, f32[4,128,128]{2,1,0:...) custom-call(f32[4,2048,256]{2,1,0:T(8,128)} %bitcast.16, f32[4,2048,256]{2,1,0:T(8,128)} %bitcast.17), custom_call_target="tpu_custom_call" | custom-call | flops 1048576 | bytes 4194304 | tf_op jit(solution)/shard_map/pack/pallas_call | solution.py:52
  29.3 2.8 %collective-permute-done.14.refs_3_ = f32[8,128,128]{2,1,0:T(8,128)} collective-permute-done((f32[8,128,128]{2,1,0:T(8,128)}, f32[8,128,128]{2,1,0:T(8,128)}, u32[]{:S(2)}, u32[]{:S(2)}) %collective-permute-start.14) | collective-permute-done | bytes 524320 | tf_op jit(solution)/shard_map/ppermute | solution.py:323
  33.2 8.7 %collective-permute-done.10.refs_2_ = f32[8,128,128]{2,1,0:T(8,128)S(1)} collective-permute-done((f32[8,128,128]{2,1,0:T(8,128)}, f32[8,128,128]{2,1,0:T(8,128)S(1)}, u32[]{:S(2)}, u32[]{:S(2)}) %collective-permute-start.10) | collective-permute-done | bytes 524320 | tf_op jit(solution)/shard_map/ppermute | solution.py:323
  41.9 2.4 %collective-permute-start.8 = (f32[8,128,128]{2,1,0:T(8,128)}, f32[8,128,128]{2,1,0:T(8,128)S(1)}, u32[]{:S(2)}, u32[]{:S(2)}) collective-permute-start(f32[8,128,128]{2,1,0:T(8,128)} %get-tuple-element.44), channel_id=1, source_target_pairs={{0,2},{1,3},{2,0},{3,1},{4,6},{5,7},{6,4},{7,5},{8,10},{9,11},{10,... | collective-permute-start | bytes 1572872 | tf_op jit(solution)/shard_map/ppermute | solution.py:323
  44.4 6.0 %gram.5 = (f32[1280,128]{1,0:T(8,128)S(1)}, f32[4,1024,64]{2,1,0:T(8,128)}) custom-call(f32[8,128,128]{2,1,0:T(8,128)S(1)} %copy-done.2, f32[8,128,128]{2,1,0:T(8,128)S(1)} %collective-permute-done.12.refs_1_, f32[8,128,128]{2,1,0:T(8,128)S(1)} %collective-permute-done.13.refs_2_, f32[8,128,128]{2,1,0:T(8,128)} %collective-permute-done.14.refs_3_, ...), custom_call_target="tpu_custom_call" | custom-call | flops 3221225472 | bytes 4194304 | tf_op jit(solution)/shard_map/gram/pallas_call | solution.py:171
  50.4 4.6 %collective-permute-start.3 = (f32[4,128,128]{2,1,0:T(8,128)S(1)}, f32[4,128,128]{2,1,0:T(8,128)S(1)}, u32[]{:S(2)}, u32[]{:S(2)}) collective-permute-start(f32[4,128,128]{2,1,0:T(8,128)S(1)} %copy-done.13), channel_id=1, source_target_pairs={{0,1},{1,2},{2,3},{3,0},{4,5},{5,6},{6,7},{7,4},{8,9},{9,10},{10,1... | collective-permute-start | bytes 786440 | tf_op jit(solution)/shard_map/ppermute | solution.py:323
  55.7 5.0 %gram.6 = (f32[1280,128]{1,0:T(8,128)S(1)}, f32[4,1024,64]{2,1,0:T(8,128)}) custom-call(f32[8,128,128]{2,1,0:T(8,128)S(1)} %copy-done.1, f32[8,128,128]{2,1,0:T(8,128)S(1)} %collective-permute-done.9.refs_1_, f32[8,128,128]{2,1,0:T(8,128)S(1)} %collective-permute-done.10.refs_2_, ...), custom_call_target="tpu_custom_call", output_to_operand_aliasing={{0}: (5, {}), {1}: (6, {})} | custom-call | flops 3221225472 | bytes 4194304 | tf_op jit(solution)/shard_map/gram/pallas_call | solution.py:171
  60.8 22.8 %collective-permute-done.3.refs_1_ = f32[4,128,128]{2,1,0:T(8,128)S(1)} collective-permute-done((f32[4,128,128]{2,1,0:T(8,128)S(1)}, f32[4,128,128]{2,1,0:T(8,128)S(1)}, u32[]{:S(2)}, u32[]{:S(2)}) %collective-permute-start.3) | collective-permute-done | bytes 262176 | tf_op jit(solution)/shard_map/ppermute | solution.py:323
  84.1 2.7 %collective-permute-start.1 = (f32[4,128,128]{2,1,0:T(8,128)S(1)}, f32[4,128,128]{2,1,0:T(8,128)S(1)}, u32[]{:S(2)}, u32[]{:S(2)}) collective-permute-start(f32[4,128,128]{2,1,0:T(8,128)S(1)} %copy-done.9), channel_id=1, source_target_pairs={{0,3},{1,0},{2,1},{3,2},{4,7},{5,4},{6,5},{7,6},{8,11},{9,8},{10,9... | collective-permute-start | bytes 786440 | tf_op jit(solution)/shard_map/ppermute | solution.py:323
  88.0 5.0 %gram.7 = (f32[1280,128]{1,0:T(8,128)S(1)}, f32[4,1024,64]{2,1,0:T(8,128)}) custom-call(f32[8,128,128]{2,1,0:T(8,128)S(1)} %copy-done, f32[8,128,128]{2,1,0:T(8,128)S(1)} %collective-permute-done.6.refs_1_, f32[8,128,128]{2,1,0:T(8,128)S(1)} %collective-permute-done.7.refs_2_, ...), custom_call_target="tpu_custom_call", output_to_operand_aliasing={{0}: (5, {}), {1}: (6, {})} | custom-call | flops 3221225472 | bytes 4194304 | tf_op jit(solution)/shard_map/gram/pallas_call | solution.py:171
  93.1 2.9 %gram.8 = (f32[1280,128]{1,0:T(8,128)S(1)}, f32[4,1024,64]{2,1,0:T(8,128)}) custom-call(f32[4,128,128]{2,1,0:T(8,128)S(1)} %copy-done.4, f32[4,128,128]{2,1,0:T(8,128)S(1)} %collective-permute-done.3.refs_1_, f32[4,128,128]{2,1,0:T(8,128)S(1)} %collective-permute-done.4.refs_2_, ...), custom_call_target="tpu_custom_call", output_to_operand_aliasing={{0}: (5, {}), {1}: (6, {})} | custom-call | flops 1610612736 | bytes 2097152 | tf_op jit(solution)/shard_map/gram/pallas_call | solution.py:171
  96.0 3.7 %collective-permute-done.refs_1_ = f32[4,128,128]{2,1,0:T(8,128)S(1)} collective-permute-done((f32[4,128,128]{2,1,0:T(8,128)S(1)}, f32[4,128,128]{2,1,0:T(8,128)S(1)}, u32[]{:S(2)}, u32[]{:S(2)}) %collective-permute-start) | collective-permute-done | bytes 262176 | tf_op jit(solution)/shard_map/ppermute | solution.py:323
  99.7 4.0 %collective-permute-done.2.refs_3_ = f32[4,128,128]{2,1,0:T(8,128)S(1)} collective-permute-done((f32[4,128,128]{2,1,0:T(8,128)S(1)}, f32[4,128,128]{2,1,0:T(8,128)S(1)}, u32[]{:S(2)}, u32[]{:S(2)}) %collective-permute-start.2) | collective-permute-done | bytes 262176 | tf_op jit(solution)/shard_map/ppermute | solution.py:323
  103.7 4.0 %gram.9 = (f32[640,128]{1,0:T(8,128)S(1)}, f32[640,128]{1,0:T(8,128)S(1)}, f32[4,1024,64]{2,1,0:T(8,128)}) custom-call(f32[4,128,128]{2,1,0:T(8,128)S(1)} %copy-done.3, f32[4,128,128]{2,1,0:T(8,128)S(1)} %collective-permute-done.refs_1_, f32[4,128,128]{2,1,0:T(8,128)S(1)} %collective-permute-done.1.refs_2_, ...), custom_call_target="tpu_custom_call", output_to_operand_aliasing={{2}: (6, {})} | custom-call | flops 1610612736 | bytes 2097152 | tf_op jit(solution)/shard_map/gram/pallas_call | solution.py:171
  110.4 16.4 %all_to_all.10 = f32[16,40,128]{2,1,0:T(8,128)S(1)} all-to-all(f32[16,40,128]{2,1,0:T(8,128)S(1)} %bitcast.20), channel_id=1, replica_groups=mesh['z'=4,'y'=4,'core'=2,'narrow'=4] {'z','y'}, dimensions={0} | all-to-all | bytes 655360 | tf_op jit(solution)/shard_map/all_to_all | solution.py:193
  126.9 2.6 %collective-permute-done.16 = f32[40,128]{1,0:T(8,128)S(1)} collective-permute-done((f32[40,128]{1,0:T(8,128)S(1)}, f32[40,128]{1,0:T(8,128)S(1)}, u32[]{:S(2)}, u32[]{:S(2)}) %collective-permute-start.16) | collective-permute-done | bytes 20512 | tf_op jit(solution)/shard_map/ppermute | solution.py:197
  129.5 3.8 %collective-permute-done.17 = f32[40,128]{1,0:T(8,128)S(1)} collective-permute-done((f32[40,128]{1,0:T(8,128)S(1)}, f32[40,128]{1,0:T(8,128)S(1)}, u32[]{:S(2)}, u32[]{:S(2)}) %collective-permute-start.17) | collective-permute-done | bytes 20512 | tf_op jit(solution)/shard_map/ppermute | solution.py:197
  133.4 10.7 %all_to_all.11 = f32[16,40,128]{2,1,0:T(8,128)S(1)} all-to-all(f32[16,40,128]{2,1,0:T(8,128)S(1)} %broadcast_in_dim.2), channel_id=1, replica_groups=mesh['z'=4,'y'=4,'core'=2,'narrow'=4] {'z','y'}, dimensions={0} | all-to-all | bytes 655360 | tf_op jit(solution)/shard_map/all_to_all | solution.py:193
  144.1 5.0 %collective-permute-start.18 = (f32[640,128]{1,0:T(8,128)S(1)}, f32[640,128]{1,0:T(8,128)S(1)}, u32[]{:S(2)}, u32[]{:S(2)}) collective-permute-start(f32[640,128]{1,0:T(8,128)S(1)} %bitcast.18), channel_id=1, source_target_pairs={{0,4},{4,0},{1,5},{5,1},{2,6},{6,2},{3,7},{7,3},{8,12},{12,8},{9,1... | collective-permute-start | bytes 983048 | tf_op jit(solution)/shard_map/ppermute | solution.py:199
  151.1 14.2 %upper_factor.1 = f32[512,512]{1,0:T(8,128)} custom-call(f32[640,128]{1,0:T(8,128)} %bitcast.19, f32[640,128]{1,0:T(8,128)} %copy-done.7), custom_call_target="tpu_custom_call" | custom-call | tf_op jit(solution)/shard_map/upper_factor/pallas_call | solution.py:301
  (59 shorter events, 17.1 us)
Async XLA Ops:
  4.7 14.7 %collective-permute-start.12 = (f32[8,128,128]{2,1,0:T(8,128)}, f32[8,128,128]{2,1,0:T(8,128)S(1)}, u32[]{:S(2)}, u32[]{:S(2)}) collective-permute-start(f32[8,128,128]{2,1,0:T(8,128)} %get-tuple-element.50), channel_id=1, source_target_pairs={{0,1},{1,2},{2,3},{3,0},{4,5},{5,6},{6,7},{7,4},{8,9},{9,10},{10,1... | collective-permute-start | bytes 1572872 | tf_op jit(solution)/shard_map/ppermute | solution.py:323
  6.7 21.3 %collective-permute-start.13 = (f32[8,128,128]{2,1,0:T(8,128)}, f32[8,128,128]{2,1,0:T(8,128)S(1)}, u32[]{:S(2)}, u32[]{:S(2)}) collective-permute-start(f32[8,128,128]{2,1,0:T(8,128)} %get-tuple-element.51), channel_id=1, source_target_pairs={{0,3},{1,0},{2,1},{3,2},{4,7},{5,4},{6,5},{7,6},{8,11},{9,8},{10,9... | collective-permute-start | bytes 1572872 | tf_op jit(solution)/shard_map/ppermute | solution.py:323
  8.1 24.0 %collective-permute-start.14 = (f32[8,128,128]{2,1,0:T(8,128)}, f32[8,128,128]{2,1,0:T(8,128)}, u32[]{:S(2)}, u32[]{:S(2)}) collective-permute-start(f32[8,128,128]{2,1,0:T(8,128)} %get-tuple-element.52), channel_id=1, source_target_pairs={{0,2},{1,3},{2,0},{3,1},{4,6},{5,7},{6,4},{7,5},{8,10},{9,11},{10,... | collective-permute-start | bytes 1572872 | tf_op jit(solution)/shard_map/ppermute | solution.py:323
  13.8 28.2 %collective-permute-start.10 = (f32[8,128,128]{2,1,0:T(8,128)}, f32[8,128,128]{2,1,0:T(8,128)S(1)}, u32[]{:S(2)}, u32[]{:S(2)}) collective-permute-start(f32[8,128,128]{2,1,0:T(8,128)} %get-tuple-element.47), channel_id=1, source_target_pairs={{0,3},{1,0},{2,1},{3,2},{4,7},{5,4},{6,5},{7,6},{8,11},{9,8},{10,9... | collective-permute-start | bytes 1572872 | tf_op jit(solution)/shard_map/ppermute | solution.py:323
  14.6 35.8 %collective-permute-start.11 = (f32[8,128,128]{2,1,0:T(8,128)}, f32[8,128,128]{2,1,0:T(8,128)S(1)}, u32[]{:S(2)}, u32[]{:S(2)}) collective-permute-start(f32[8,128,128]{2,1,0:T(8,128)} %get-tuple-element.48), channel_id=1, source_target_pairs={{0,2},{1,3},{2,0},{3,1},{4,6},{5,7},{6,4},{7,5},{8,10},{9,11},{10,... | collective-permute-start | bytes 1572872 | tf_op jit(solution)/shard_map/ppermute | solution.py:323
  19.4 36.1 %collective-permute-start.9 = (f32[8,128,128]{2,1,0:T(8,128)}, f32[8,128,128]{2,1,0:T(8,128)S(1)}, u32[]{:S(2)}, u32[]{:S(2)}) collective-permute-start(f32[8,128,128]{2,1,0:T(8,128)} %get-tuple-element.46), channel_id=1, source_target_pairs={{0,1},{1,2},{2,3},{3,0},{4,5},{5,6},{6,7},{7,4},{8,9},{9,10},{10,1... | collective-permute-start | bytes 1572872 | tf_op jit(solution)/shard_map/ppermute | solution.py:323
  28.0 56.0 %collective-permute-start.6 = (f32[8,128,128]{2,1,0:T(8,128)}, f32[8,128,128]{2,1,0:T(8,128)S(1)}, u32[]{:S(2)}, u32[]{:S(2)}) collective-permute-start(f32[8,128,128]{2,1,0:T(8,128)} %get-tuple-element.42), channel_id=1, source_target_pairs={{0,1},{1,2},{2,3},{3,0},{4,5},{5,6},{6,7},{7,4},{8,9},{9,10},{10,1... | collective-permute-start | bytes 1572872 | tf_op jit(solution)/shard_map/ppermute | solution.py:323
  32.1 51.9 %collective-permute-start.7 = (f32[8,128,128]{2,1,0:T(8,128)}, f32[8,128,128]{2,1,0:T(8,128)S(1)}, u32[]{:S(2)}, u32[]{:S(2)}) collective-permute-start(f32[8,128,128]{2,1,0:T(8,128)} %get-tuple-element.43), channel_id=1, source_target_pairs={{0,3},{1,0},{2,1},{3,2},{4,7},{5,4},{6,5},{7,6},{8,11},{9,8},{10,9... | collective-permute-start | bytes 1572872 | tf_op jit(solution)/shard_map/ppermute | solution.py:323
  41.9 44.8 %collective-permute-start.8 = (f32[8,128,128]{2,1,0:T(8,128)}, f32[8,128,128]{2,1,0:T(8,128)S(1)}, u32[]{:S(2)}, u32[]{:S(2)}) collective-permute-start(f32[8,128,128]{2,1,0:T(8,128)} %get-tuple-element.44), channel_id=1, source_target_pairs={{0,2},{1,3},{2,0},{3,1},{4,6},{5,7},{6,4},{7,5},{8,10},{9,11},{10,... | collective-permute-start | bytes 1572872 | tf_op jit(solution)/shard_map/ppermute | solution.py:323
  50.4 33.1 %collective-permute-start.3 = (f32[4,128,128]{2,1,0:T(8,128)S(1)}, f32[4,128,128]{2,1,0:T(8,128)S(1)}, u32[]{:S(2)}, u32[]{:S(2)}) collective-permute-start(f32[4,128,128]{2,1,0:T(8,128)S(1)} %copy-done.13), channel_id=1, source_target_pairs={{0,1},{1,2},{2,3},{3,0},{4,5},{5,6},{6,7},{7,4},{8,9},{9,10},{10,1... | collective-permute-start | bytes 786440 | tf_op jit(solution)/shard_map/ppermute | solution.py:323
  55.5 37.6 %collective-permute-start.4 = (f32[4,128,128]{2,1,0:T(8,128)S(1)}, f32[4,128,128]{2,1,0:T(8,128)S(1)}, u32[]{:S(2)}, u32[]{:S(2)}) collective-permute-start(f32[4,128,128]{2,1,0:T(8,128)S(1)} %copy-done.12), channel_id=1, source_target_pairs={{0,3},{1,0},{2,1},{3,2},{4,7},{5,4},{6,5},{7,6},{8,11},{9,8},{10,9... | collective-permute-start | bytes 786440 | tf_op jit(solution)/shard_map/ppermute | solution.py:323
  55.7 27.9 %copy-start.11 = (f32[4,128,128]{2,1,0:T(8,128)S(1)}, f32[4,128,128]{2,1,0:T(8,128)}, u32[]{:S(2)}) copy-start(f32[4,128,128]{2,1,0:T(8,128)} %get-tuple-element.40) | copy-start | bytes 786436
  55.7 28.3 %copy-start.10 = (f32[4,128,128]{2,1,0:T(8,128)S(1)}, f32[4,128,128]{2,1,0:T(8,128)}, u32[]{:S(2)}) copy-start(f32[4,128,128]{2,1,0:T(8,128)} %get-tuple-element.34) | copy-start | bytes 786436
  55.7 28.3 %copy-start.9 = (f32[4,128,128]{2,1,0:T(8,128)S(1)}, f32[4,128,128]{2,1,0:T(8,128)}, u32[]{:S(2)}) copy-start(f32[4,128,128]{2,1,0:T(8,128)} %get-tuple-element.35) | copy-start | bytes 786436
  55.7 31.0 %copy-start.8 = (f32[4,128,128]{2,1,0:T(8,128)S(1)}, f32[4,128,128]{2,1,0:T(8,128)}, u32[]{:S(2)}) copy-start(f32[4,128,128]{2,1,0:T(8,128)} %get-tuple-element.36) | copy-start | bytes 786436
  55.7 32.3 %copy-start = (f32[8,128,128]{2,1,0:T(8,128)S(1)}, f32[8,128,128]{2,1,0:T(8,128)}, u32[]{:S(2)}) copy-start(f32[8,128,128]{2,1,0:T(8,128)} %get-tuple-element.41.refs_0_) | copy-start | bytes 1572868
  83.6 9.5 %collective-permute-start.5 = (f32[4,128,128]{2,1,0:T(8,128)S(1)}, f32[4,128,128]{2,1,0:T(8,128)S(1)}, u32[]{:S(2)}, u32[]{:S(2)}) collective-permute-start(f32[4,128,128]{2,1,0:T(8,128)S(1)} %copy-done.11), channel_id=1, source_target_pairs={{0,2},{1,3},{2,0},{3,1},{4,6},{5,7},{6,4},{7,5},{8,10},{9,11},{10,... | collective-permute-start | bytes 786440 | tf_op jit(solution)/shard_map/ppermute | solution.py:323
  84.0 15.7 %collective-permute-start = (f32[4,128,128]{2,1,0:T(8,128)S(1)}, f32[4,128,128]{2,1,0:T(8,128)S(1)}, u32[]{:S(2)}, u32[]{:S(2)}) collective-permute-start(f32[4,128,128]{2,1,0:T(8,128)S(1)} %copy-done.10), channel_id=1, source_target_pairs={{0,1},{1,2},{2,3},{3,0},{4,5},{5,6},{6,7},{7,4},{8,9},{9,10},{10,1... | collective-permute-start | bytes 786440 | tf_op jit(solution)/shard_map/ppermute | solution.py:323
  84.1 15.7 %collective-permute-start.1 = (f32[4,128,128]{2,1,0:T(8,128)S(1)}, f32[4,128,128]{2,1,0:T(8,128)S(1)}, u32[]{:S(2)}, u32[]{:S(2)}) collective-permute-start(f32[4,128,128]{2,1,0:T(8,128)S(1)} %copy-done.9), channel_id=1, source_target_pairs={{0,3},{1,0},{2,1},{3,2},{4,7},{5,4},{6,5},{7,6},{8,11},{9,8},{10,9... | collective-permute-start | bytes 786440 | tf_op jit(solution)/shard_map/ppermute | solution.py:323
  86.7 17.0 %collective-permute-start.2 = (f32[4,128,128]{2,1,0:T(8,128)S(1)}, f32[4,128,128]{2,1,0:T(8,128)S(1)}, u32[]{:S(2)}, u32[]{:S(2)}) collective-permute-start(f32[4,128,128]{2,1,0:T(8,128)S(1)} %copy-done.8), channel_id=1, source_target_pairs={{0,2},{1,3},{2,0},{3,1},{4,6},{5,7},{6,4},{7,5},{8,10},{9,11},{10,... | collective-permute-start | bytes 786440 | tf_op jit(solution)/shard_map/ppermute | solution.py:323
  107.8 2.6 %collective-permute-start.15 = (f32[640,128]{1,0:T(8,128)S(1)}, f32[640,128]{1,0:T(8,128)S(1)}, u32[]{:S(2)}, u32[]{:S(2)}) collective-permute-start(f32[640,128]{1,0:T(8,128)S(1)} %get-tuple-element.62), channel_id=1, source_target_pairs={{0,4},{4,0},{1,5},{5,1},{2,6},{6,2},{3,7},{7,3},{8,12},{12,8},{9,1... | collective-permute-start | bytes 983048 | tf_op jit(solution)/shard_map/ppermute | solution.py:191
  126.8 2.7 %collective-permute-start.16 = (f32[40,128]{1,0:T(8,128)S(1)}, f32[40,128]{1,0:T(8,128)S(1)}, u32[]{:S(2)}, u32[]{:S(2)}) collective-permute-start(f32[40,128]{1,0:T(8,128)S(1)} %reduce_sum.9), channel_id=1, source_target_pairs={{0,1},{1,0},{2,3},{3,2},{4,5},{5,4},{6,7},{7,6},{8,9},{9,8},{10,11... | collective-permute-start | bytes 61448 | tf_op jit(solution)/shard_map/ppermute | solution.py:197
  129.5 3.8 %collective-permute-start.17 = (f32[40,128]{1,0:T(8,128)S(1)}, f32[40,128]{1,0:T(8,128)S(1)}, u32[]{:S(2)}, u32[]{:S(2)}) collective-permute-start(f32[40,128]{1,0:T(8,128)S(1)} %add.10), channel_id=1, source_target_pairs={{0,3},{1,2},{2,1},{3,0},{4,7},{5,6},{6,5},{7,4},{8,11},{9,10},{10,... | collective-permute-start | bytes 61448 | tf_op jit(solution)/shard_map/ppermute | solution.py:197
  144.1 6.3 %collective-permute-start.18 = (f32[640,128]{1,0:T(8,128)S(1)}, f32[640,128]{1,0:T(8,128)S(1)}, u32[]{:S(2)}, u32[]{:S(2)}) collective-permute-start(f32[640,128]{1,0:T(8,128)S(1)} %bitcast.18), channel_id=1, source_target_pairs={{0,4},{4,0},{1,5},{5,1},{2,6},{6,2},{3,7},{7,3},{8,12},{12,8},{9,1... | collective-permute-start | bytes 983048 | tf_op jit(solution)/shard_map/ppermute | solution.py:199
  (9 other events, 92.3 us)

commit v2 on v1

--- a/solution.py
+++ b/solution.py
@@ -11,7 +11,7 @@
 SHIFTS = (1, 3, 2)
 FULL = [(0, 8)]
 HALVES = [(0, 4), (4, 4)]
-PLAN = [(0, FULL), (1, FULL), (2, FULL), (3, HALVES)]
+PLAN = [(0, FULL), (1, FULL), (2, FULL), (3, [(0, 6), (6, 2)])]
 HALF = 640
 WIDE = ("z", "y", "core")
 PANEL = 8
@@ -150,7 +150,7 @@
     first = acc is None
     merge = base > 0
     depth = pieces[0].shape[0]
-    take = min(depth, 4)
+    take = 2 if depth < 4 else depth // 2
     piece_spec = pl.BlockSpec((take, 128, 128), lambda s: (s, 0, 0))
     whole = lambda s: (0, 0)
     in_specs = [piece_spec] * 4 + [pl.BlockSpec((64, 512), whole)]

time: 166 us -> 161 us (0.970)
  waiting for transfers between devices: 55 us -> 47 us
  local copies, waits for them, and re-layouts: 0.81 us -> 2.69 us
    ppermute x15, waiting for transfers between devices: 46 us -> 41.3 us  [on_device(): arrived.append([lax.ppermute(p[k], 'narrow', ring(4, k)) for k in SHIFTS])]
    ppermute x15, starting transfers between devices: 21.6 us -> 18.3 us  [on_device(): arrived.append([lax.ppermute(p[k], 'narrow', ring(4, k)) for k in SHIFTS])]
    ppermute x2, starting transfers between devices: 0.09 us -> 3.35 us  [total(): piece += lax.ppermute(piece, 'narrow', [(i, i ^ flip) for i in range(4)])]
    ppermute x2, waiting for transfers between devices: 6.46 us -> 3.21 us  [total(): piece += lax.ppermute(piece, 'narrow', [(i, i ^ flip) for i in range(4)])]
    unnamed x28 -> x32, local copies, waits for them, and re-layouts: 0.79 us -> 2.66 us
  transfers between devices with their start and end apart: 19 -> 19, of which waited for: 11 -> 12; matrix products, arithmetic and copies ran while one was open for 0% -> 0% of each run, Pallas kernels for 19% -> 21%
where the time goes in v2:
time: 161 us
  Pallas kernels  54.5 us (34%)
  waiting for transfers between devices  47 us (29%)
  starting transfers between devices  28.7 us (18%)
  blocking collectives  27.1 us (17%)
  local copies, waits for them, and re-layouts  2.69 us (2%)
    ppermute x15, waiting for transfers between devices, on_device(): arrived.append([lax.ppermute(p[k], 'narrow', ring(4, k)) for k in SHIFTS])  41.3 us
    all_to_all x2, blocking collectives, total(): deal = lambda x, axes: lax.all_to_all(x, axes, 0, 0, tiled=True)  27.1 us
    pallas_call x5, Pallas kernels, gram_step(): pl.pallas_call(functools.partial(gram_kernel, first, last, merge, base),...  24 us
    ppermute x15, starting transfers between devices, on_device(): arrived.append([lax.ppermute(p[k], 'narrow', ring(4, k)) for k in SHIFTS])  18.3 us
    pallas_call x4, Pallas kernels, pack(): pl.pallas_call(functools.partial(pack_kernel, ranges), grid=(2,), in_spec...  16.3 us
    pallas_call x1, Pallas kernels, upper_factor(): pl.pallas_call(functools.partial(chol_kernel, scale), out_shape=jax.Shape...  14.2 us
    ppermute x1, starting transfers between devices, total(): return (h, lax.ppermute(h, 'core', swap))  5.03 us
    ppermute x2, starting transfers between devices, total(): piece += lax.ppermute(piece, 'narrow', [(i, i ^ flip) for i in range(4)])  3.35 us
  transfers between devices with their start and end apart: 19, of which 12 were waited for; matrix products, arithmetic and copies ran while one was open for 0% of the time, Pallas kernels for 21%

profile of v2, /device:TPU:1, one launch (start us, length us, event | category | flops | bytes accessed | tf_op | source)
XLA Modules:
  0.0 160.7 jit_solution(17620452666842264306)
XLA Ops:
  0.6 4.1 %pack.7 = (f32[8,128,128]{2,1,0:T(8,128)}, f32[8,128,128]{2,1,0:T(8,128)}, f32[8,128,128]{2,1,0:T(8,128)}, f32[8,128,128]{2,1,0:T(8,128)}) custom-call(f32[4,2048,256]{2,1,0:T(8,128)} %bitcast.10, f32[4,2048,256]{2,1,0:T(8,128)} %bitcast.11), custom_call_target="tpu_custom_call" | custom-call | flops 1048576 | bytes 4194304 | tf_op jit(solution)/shard_map/pack/pallas_call | solution.py:52
  4.7 2.0 %collective-permute-start.12 = (f32[8,128,128]{2,1,0:T(8,128)}, f32[8,128,128]{2,1,0:T(8,128)S(1)}, u32[]{:S(2)}, u32[]{:S(2)}) collective-permute-start(f32[8,128,128]{2,1,0:T(8,128)} %get-tuple-element.50), channel_id=1, source_target_pairs={{0,1},{1,2},{2,3},{3,0},{4,5},{5,6},{6,7},{7,4},{8,9},{9,10},{10,1... | collective-permute-start | bytes 1572872 | tf_op jit(solution)/shard_map/ppermute | solution.py:323
  9.7 4.1 %pack.6 = (f32[8,128,128]{2,1,0:T(8,128)}, f32[8,128,128]{2,1,0:T(8,128)}, f32[8,128,128]{2,1,0:T(8,128)}, f32[8,128,128]{2,1,0:T(8,128)}) custom-call(f32[4,2048,256]{2,1,0:T(8,128)} %bitcast.12, f32[4,2048,256]{2,1,0:T(8,128)} %bitcast.13), custom_call_target="tpu_custom_call" | custom-call | flops 1048576 | bytes 4194304 | tf_op jit(solution)/shard_map/pack/pallas_call | solution.py:52
  15.9 4.0 %pack.5 = (f32[8,128,128]{2,1,0:T(8,128)}, f32[8,128,128]{2,1,0:T(8,128)}, f32[8,128,128]{2,1,0:T(8,128)}, f32[8,128,128]{2,1,0:T(8,128)}) custom-call(f32[4,2048,256]{2,1,0:T(8,128)} %bitcast.14, f32[4,2048,256]{2,1,0:T(8,128)} %bitcast.15), custom_call_target="tpu_custom_call" | custom-call | flops 1048576 | bytes 4194304 | tf_op jit(solution)/shard_map/pack/pallas_call | solution.py:52
  22.2 4.1 %pack.4 = (f32[6,128,128]{2,1,0:T(8,128)}, f32[6,128,128]{2,1,0:T(8,128)}, f32[6,128,128]{2,1,0:T(8,128)}, f32[6,128,128]{2,1,0:T(8,128)}, f32[2,128,128]{2,1,0:...) custom-call(f32[4,2048,256]{2,1,0:T(8,128)} %bitcast.16, f32[4,2048,256]{2,1,0:T(8,128)} %bitcast.17), custom_call_target="tpu_custom_call" | custom-call | flops 1048576 | bytes 4194304 | tf_op jit(solution)/shard_map/pack/pallas_call | solution.py:52
  26.3 5.7 %collective-permute-done.14.refs_3_ = f32[8,128,128]{2,1,0:T(8,128)} collective-permute-done((f32[8,128,128]{2,1,0:T(8,128)}, f32[8,128,128]{2,1,0:T(8,128)}, u32[]{:S(2)}, u32[]{:S(2)}) %collective-permute-start.14) | collective-permute-done | bytes 524320 | tf_op jit(solution)/shard_map/ppermute | solution.py:323
  33.2 8.7 %collective-permute-done.10.refs_2_ = f32[8,128,128]{2,1,0:T(8,128)S(1)} collective-permute-done((f32[8,128,128]{2,1,0:T(8,128)}, f32[8,128,128]{2,1,0:T(8,128)S(1)}, u32[]{:S(2)}, u32[]{:S(2)}) %collective-permute-start.10) | collective-permute-done | bytes 524320 | tf_op jit(solution)/shard_map/ppermute | solution.py:323
  41.9 2.4 %collective-permute-start.8 = (f32[8,128,128]{2,1,0:T(8,128)}, f32[8,128,128]{2,1,0:T(8,128)S(1)}, u32[]{:S(2)}, u32[]{:S(2)}) collective-permute-start(f32[8,128,128]{2,1,0:T(8,128)} %get-tuple-element.44), channel_id=1, source_target_pairs={{0,2},{1,3},{2,0},{3,1},{4,6},{5,7},{6,4},{7,5},{8,10},{9,11},{10,... | collective-permute-start | bytes 1572872 | tf_op jit(solution)/shard_map/ppermute | solution.py:323
  45.4 6.1 %gram.5 = (f32[1280,128]{1,0:T(8,128)S(1)}, f32[4,1024,64]{2,1,0:T(8,128)}) custom-call(f32[8,128,128]{2,1,0:T(8,128)S(1)} %copy-done.4, f32[8,128,128]{2,1,0:T(8,128)S(1)} %collective-permute-done.12.refs_1_, f32[8,128,128]{2,1,0:T(8,128)S(1)} %copy-done.6, f32[8,128,128]{2,1,0:T(8,128)} %collective-permute-done.14.refs_3_, f32[64,512]{1,0:T(8,128)S(1)} %bitcast.5), custom_call_target="tpu_custom_call" | custom-call | flops 3221225472 | bytes 4194304 | tf_op jit(solution)/shard_map/gram/pallas_call | solution.py:171
  51.5 3.5 %collective-permute-start.3 = (f32[6,128,128]{2,1,0:T(8,128)S(1)}, f32[6,128,128]{2,1,0:T(8,128)S(1)}, u32[]{:S(2)}, u32[]{:S(2)}) collective-permute-start(f32[6,128,128]{2,1,0:T(8,128)S(1)} %copy-done.12), channel_id=1, source_target_pairs={{0,1},{1,2},{2,3},{3,0},{4,5},{5,6},{6,7},{7,4},{8,9},{9,10},{10,1... | collective-permute-start | bytes 1179656 | tf_op jit(solution)/shard_map/ppermute | solution.py:323
  55.7 12.0 %collective-permute-done.6.refs_1_ = f32[8,128,128]{2,1,0:T(8,128)S(1)} collective-permute-done((f32[8,128,128]{2,1,0:T(8,128)}, f32[8,128,128]{2,1,0:T(8,128)S(1)}, u32[]{:S(2)}, u32[]{:S(2)}) %collective-permute-start.6) | collective-permute-done | bytes 524320 | tf_op jit(solution)/shard_map/ppermute | solution.py:323
  68.3 5.1 %gram.6 = (f32[1280,128]{1,0:T(8,128)S(1)}, f32[4,1024,64]{2,1,0:T(8,128)}) custom-call(f32[8,128,128]{2,1,0:T(8,128)S(1)} %copy-done.3, f32[8,128,128]{2,1,0:T(8,128)S(1)} %collective-permute-done.9.refs_1_, f32[8,128,128]{2,1,0:T(8,128)S(1)} %collective-permute-done.10.refs_2_, ...), custom_call_target="tpu_custom_call", output_to_operand_aliasing={{0}: (5, {}), {1}: (6, {})} | custom-call | flops 3221225472 | bytes 4194304 | tf_op jit(solution)/shard_map/gram/pallas_call | solution.py:171
  73.4 3.6 %collective-permute-done.8.refs_3_ = f32[8,128,128]{2,1,0:T(8,128)S(1)} collective-permute-done((f32[8,128,128]{2,1,0:T(8,128)}, f32[8,128,128]{2,1,0:T(8,128)S(1)}, u32[]{:S(2)}, u32[]{:S(2)}) %collective-permute-start.8) | collective-permute-done | bytes 524320 | tf_op jit(solution)/shard_map/ppermute | solution.py:323
  78.1 5.0 %gram.7 = (f32[1280,128]{1,0:T(8,128)S(1)}, f32[4,1024,64]{2,1,0:T(8,128)}) custom-call(f32[8,128,128]{2,1,0:T(8,128)S(1)} %copy-done.2, f32[8,128,128]{2,1,0:T(8,128)S(1)} %collective-permute-done.6.refs_1_, f32[8,128,128]{2,1,0:T(8,128)S(1)} %collective-permute-done.7.refs_2_, ...), custom_call_target="tpu_custom_call", output_to_operand_aliasing={{0}: (5, {}), {1}: (6, {})} | custom-call | flops 3221225472 | bytes 4194304 | tf_op jit(solution)/shard_map/gram/pallas_call | solution.py:171
  83.1 4.0 %collective-permute-done.3.refs_1_ = f32[6,128,128]{2,1,0:T(8,128)S(1)} collective-permute-done((f32[6,128,128]{2,1,0:T(8,128)S(1)}, f32[6,128,128]{2,1,0:T(8,128)S(1)}, u32[]{:S(2)}, u32[]{:S(2)}) %collective-permute-start.3) | collective-permute-done | bytes 393248 | tf_op jit(solution)/shard_map/ppermute | solution.py:323
  87.7 6.1 %collective-permute-done.5.refs_3_ = f32[6,128,128]{2,1,0:T(8,128)S(1)} collective-permute-done((f32[6,128,128]{2,1,0:T(8,128)S(1)}, f32[6,128,128]{2,1,0:T(8,128)S(1)}, u32[]{:S(2)}, u32[]{:S(2)}) %collective-permute-start.5) | collective-permute-done | bytes 393248 | tf_op jit(solution)/shard_map/ppermute | solution.py:323
  93.9 4.8 %gram.8 = (f32[1280,128]{1,0:T(8,128)S(1)}, f32[4,1024,64]{2,1,0:T(8,128)}) custom-call(f32[6,128,128]{2,1,0:T(8,128)S(1)} %copy-done.7, f32[6,128,128]{2,1,0:T(8,128)S(1)} %collective-permute-done.3.refs_1_, f32[6,128,128]{2,1,0:T(8,128)S(1)} %collective-permute-done.4.refs_2_, ...), custom_call_target="tpu_custom_call", output_to_operand_aliasing={{0}: (5, {}), {1}: (6, {})} | custom-call | flops 2415919104 | bytes 3145728 | tf_op jit(solution)/shard_map/gram/pallas_call | solution.py:171
  99.3 3.1 %gram.9 = (f32[640,128]{1,0:T(8,128)S(1)}, f32[640,128]{1,0:T(8,128)S(1)}, f32[4,1024,64]{2,1,0:T(8,128)}) custom-call(f32[2,128,128]{2,1,0:T(8,128)S(1)} %copy-done.1, f32[2,128,128]{2,1,0:T(8,128)S(1)} %collective-permute-done.refs_1_, f32[2,128,128]{2,1,0:T(8,128)S(1)} %collective-permute-done.1.refs_2_, ...), custom_call_target="tpu_custom_call", output_to_operand_aliasing={{2}: (6, {})} | custom-call | flops 805306368 | bytes 1048576 | tf_op jit(solution)/shard_map/gram/pallas_call | solution.py:171
  102.4 2.0 %collective-permute-start.15 = (f32[640,128]{1,0:T(8,128)S(1)}, f32[640,128]{1,0:T(8,128)S(1)}, u32[]{:S(2)}, u32[]{:S(2)}) collective-permute-start(f32[640,128]{1,0:T(8,128)S(1)} %get-tuple-element.62), channel_id=1, source_target_pairs={{0,4},{4,0},{1,5},{5,1},{2,6},{6,2},{3,7},{7,3},{8,12},{12,8},{9,1... | collective-permute-start | bytes 983048 | tf_op jit(solution)/shard_map/ppermute | solution.py:191
  105.7 16.4 %all_to_all.10 = f32[16,40,128]{2,1,0:T(8,128)S(1)} all-to-all(f32[16,40,128]{2,1,0:T(8,128)S(1)} %bitcast.21), channel_id=1, replica_groups=mesh['z'=4,'y'=4,'core'=2,'narrow'=4] {'z','y'}, dimensions={0} | all-to-all | bytes 655360 | tf_op jit(solution)/shard_map/all_to_all | solution.py:193
  124.8 2.0 %collective-permute-start.17 = (f32[40,128]{1,0:T(8,128)S(1)}, f32[40,128]{1,0:T(8,128)S(1)}, u32[]{:S(2)}, u32[]{:S(2)}) collective-permute-start(f32[40,128]{1,0:T(8,128)S(1)} %add.10), channel_id=1, source_target_pairs={{0,3},{1,2},{2,1},{3,0},{4,7},{5,6},{6,5},{7,4},{8,11},{9,10},{10,... | collective-permute-start | bytes 61448 | tf_op jit(solution)/shard_map/ppermute | solution.py:197
  128.7 10.7 %all_to_all.11 = f32[16,40,128]{2,1,0:T(8,128)S(1)} all-to-all(f32[16,40,128]{2,1,0:T(8,128)S(1)} %broadcast_in_dim.2), channel_id=1, replica_groups=mesh['z'=4,'y'=4,'core'=2,'narrow'=4] {'z','y'}, dimensions={0} | all-to-all | bytes 655360 | tf_op jit(solution)/shard_map/all_to_all | solution.py:193
  139.4 5.0 %collective-permute-start.18 = (f32[640,128]{1,0:T(8,128)S(1)}, f32[640,128]{1,0:T(8,128)S(1)}, u32[]{:S(2)}, u32[]{:S(2)}) collective-permute-start(f32[640,128]{1,0:T(8,128)S(1)} %bitcast.19), channel_id=1, source_target_pairs={{0,4},{4,0},{1,5},{5,1},{2,6},{6,2},{3,7},{7,3},{8,12},{12,8},{9,1... | collective-permute-start | bytes 983048 | tf_op jit(solution)/shard_map/ppermute | solution.py:199
  146.4 14.2 %upper_factor.1 = f32[512,512]{1,0:T(8,128)} custom-call(f32[640,128]{1,0:T(8,128)} %bitcast.20, f32[640,128]{1,0:T(8,128)} %copy-done.9), custom_call_target="tpu_custom_call" | custom-call | tf_op jit(solution)/shard_map/upper_factor/pallas_call | solution.py:301
  (63 shorter events, 21.2 us)
Async XLA Ops:
  4.7 15.2 %collective-permute-start.12 = (f32[8,128,128]{2,1,0:T(8,128)}, f32[8,128,128]{2,1,0:T(8,128)S(1)}, u32[]{:S(2)}, u32[]{:S(2)}) collective-permute-start(f32[8,128,128]{2,1,0:T(8,128)} %get-tuple-element.50), channel_id=1, source_target_pairs={{0,1},{1,2},{2,3},{3,0},{4,5},{5,6},{6,7},{7,4},{8,9},{9,10},{10,1... | collective-permute-start | bytes 1572872 | tf_op jit(solution)/shard_map/ppermute | solution.py:323
  6.7 13.3 %collective-permute-start.13 = (f32[8,128,128]{2,1,0:T(8,128)}, f32[8,128,128]{2,1,0:T(8,128)S(1)}, u32[]{:S(2)}, u32[]{:S(2)}) collective-permute-start(f32[8,128,128]{2,1,0:T(8,128)} %get-tuple-element.51), channel_id=1, source_target_pairs={{0,3},{1,0},{2,1},{3,2},{4,7},{5,4},{6,5},{7,6},{8,11},{9,8},{10,9... | collective-permute-start | bytes 1572872 | tf_op jit(solution)/shard_map/ppermute | solution.py:323
  8.0 24.0 %collective-permute-start.14 = (f32[8,128,128]{2,1,0:T(8,128)}, f32[8,128,128]{2,1,0:T(8,128)}, u32[]{:S(2)}, u32[]{:S(2)}) collective-permute-start(f32[8,128,128]{2,1,0:T(8,128)} %get-tuple-element.52), channel_id=1, source_target_pairs={{0,2},{1,3},{2,0},{3,1},{4,6},{5,7},{6,4},{7,5},{8,10},{9,11},{10,... | collective-permute-start | bytes 1572872 | tf_op jit(solution)/shard_map/ppermute | solution.py:323
  13.8 28.2 %collective-permute-start.10 = (f32[8,128,128]{2,1,0:T(8,128)}, f32[8,128,128]{2,1,0:T(8,128)S(1)}, u32[]{:S(2)}, u32[]{:S(2)}) collective-permute-start(f32[8,128,128]{2,1,0:T(8,128)} %get-tuple-element.47), channel_id=1, source_target_pairs={{0,3},{1,0},{2,1},{3,2},{4,7},{5,4},{6,5},{7,6},{8,11},{9,8},{10,9... | collective-permute-start | bytes 1572872 | tf_op jit(solution)/shard_map/ppermute | solution.py:323
  14.6 36.9 %collective-permute-start.11 = (f32[8,128,128]{2,1,0:T(8,128)}, f32[8,128,128]{2,1,0:T(8,128)S(1)}, u32[]{:S(2)}, u32[]{:S(2)}) collective-permute-start(f32[8,128,128]{2,1,0:T(8,128)} %get-tuple-element.48), channel_id=1, source_target_pairs={{0,2},{1,3},{2,0},{3,1},{4,6},{5,7},{6,4},{7,5},{8,10},{9,11},{10,... | collective-permute-start | bytes 1572872 | tf_op jit(solution)/shard_map/ppermute | solution.py:323
  19.9 35.6 %collective-permute-start.9 = (f32[8,128,128]{2,1,0:T(8,128)}, f32[8,128,128]{2,1,0:T(8,128)S(1)}, u32[]{:S(2)}, u32[]{:S(2)}) collective-permute-start(f32[8,128,128]{2,1,0:T(8,128)} %get-tuple-element.46), channel_id=1, source_target_pairs={{0,1},{1,2},{2,3},{3,0},{4,5},{5,6},{6,7},{7,4},{8,9},{9,10},{10,1... | collective-permute-start | bytes 1572872 | tf_op jit(solution)/shard_map/ppermute | solution.py:323
  20.8 23.5 %copy-start = (f32[512,64]{0,1:T(8,128)S(1)}, f32[512,64]{0,1:T(8,128)}, u32[]{:S(2)}) copy-start(f32[512,64]{0,1:T(8,128)} %param.3) | copy-start | bytes 393220
  20.8 23.5 %copy-start.4 = (f32[8,128,128]{2,1,0:T(8,128)S(1)}, f32[8,128,128]{2,1,0:T(8,128)}, u32[]{:S(2)}) copy-start(f32[8,128,128]{2,1,0:T(8,128)} %get-tuple-element.49.refs_0_) | copy-start | bytes 1572868
  20.8 46.9 %collective-permute-start.6 = (f32[8,128,128]{2,1,0:T(8,128)}, f32[8,128,128]{2,1,0:T(8,128)S(1)}, u32[]{:S(2)}, u32[]{:S(2)}) collective-permute-start(f32[8,128,128]{2,1,0:T(8,128)} %get-tuple-element.42), channel_id=1, source_target_pairs={{0,1},{1,2},{2,3},{3,0},{4,5},{5,6},{6,7},{7,4},{8,9},{9,10},{10,1... | collective-permute-start | bytes 1572872 | tf_op jit(solution)/shard_map/ppermute | solution.py:323
  32.1 41.3 %collective-permute-start.7 = (f32[8,128,128]{2,1,0:T(8,128)}, f32[8,128,128]{2,1,0:T(8,128)S(1)}, u32[]{:S(2)}, u32[]{:S(2)}) collective-permute-start(f32[8,128,128]{2,1,0:T(8,128)} %get-tuple-element.43), channel_id=1, source_target_pairs={{0,3},{1,0},{2,1},{3,2},{4,7},{5,4},{6,5},{7,6},{8,11},{9,8},{10,9... | collective-permute-start | bytes 1572872 | tf_op jit(solution)/shard_map/ppermute | solution.py:323
  41.9 35.0 %collective-permute-start.8 = (f32[8,128,128]{2,1,0:T(8,128)}, f32[8,128,128]{2,1,0:T(8,128)S(1)}, u32[]{:S(2)}, u32[]{:S(2)}) collective-permute-start(f32[8,128,128]{2,1,0:T(8,128)} %get-tuple-element.44), channel_id=1, source_target_pairs={{0,2},{1,3},{2,0},{3,1},{4,6},{5,7},{6,4},{7,5},{8,10},{9,11},{10,... | collective-permute-start | bytes 1572872 | tf_op jit(solution)/shard_map/ppermute | solution.py:323
  45.4 22.3 %copy-start.10 = (f32[6,128,128]{2,1,0:T(8,128)S(1)}, f32[6,128,128]{2,1,0:T(8,128)}, u32[]{:S(2)}) copy-start(f32[6,128,128]{2,1,0:T(8,128)} %get-tuple-element.40) | copy-start | bytes 1179652
  45.4 22.9 %copy-start.3 = (f32[8,128,128]{2,1,0:T(8,128)S(1)}, f32[8,128,128]{2,1,0:T(8,128)}, u32[]{:S(2)}) copy-start(f32[8,128,128]{2,1,0:T(8,128)} %get-tuple-element.45.refs_0_) | copy-start | bytes 1572868
  51.5 35.6 %collective-permute-start.3 = (f32[6,128,128]{2,1,0:T(8,128)S(1)}, f32[6,128,128]{2,1,0:T(8,128)S(1)}, u32[]{:S(2)}, u32[]{:S(2)}) collective-permute-start(f32[6,128,128]{2,1,0:T(8,128)S(1)} %copy-done.12), channel_id=1, source_target_pairs={{0,1},{1,2},{2,3},{3,0},{4,5},{5,6},{6,7},{7,4},{8,9},{9,10},{10,1... | collective-permute-start | bytes 1179656 | tf_op jit(solution)/shard_map/ppermute | solution.py:323
  55.5 32.3 %collective-permute-start.4 = (f32[6,128,128]{2,1,0:T(8,128)S(1)}, f32[6,128,128]{2,1,0:T(8,128)S(1)}, u32[]{:S(2)}, u32[]{:S(2)}) collective-permute-start(f32[6,128,128]{2,1,0:T(8,128)S(1)} %copy-done.11), channel_id=1, source_target_pairs={{0,3},{1,0},{2,1},{3,2},{4,7},{5,4},{6,5},{7,6},{8,11},{9,8},{10,9... | collective-permute-start | bytes 1179656 | tf_op jit(solution)/shard_map/ppermute | solution.py:323
  67.7 26.2 %collective-permute-start.5 = (f32[6,128,128]{2,1,0:T(8,128)S(1)}, f32[6,128,128]{2,1,0:T(8,128)S(1)}, u32[]{:S(2)}, u32[]{:S(2)}) collective-permute-start(f32[6,128,128]{2,1,0:T(8,128)S(1)} %copy-done.10), channel_id=1, source_target_pairs={{0,2},{1,3},{2,0},{3,1},{4,6},{5,7},{6,4},{7,5},{8,10},{9,11},{10,... | collective-permute-start | bytes 1179656 | tf_op jit(solution)/shard_map/ppermute | solution.py:323
  73.4 25.2 %collective-permute-start = (f32[2,128,128]{2,1,0:T(8,128)S(1)}, f32[2,128,128]{2,1,0:T(8,128)S(1)}, u32[]{:S(2)}, u32[]{:S(2)}) collective-permute-start(f32[2,128,128]{2,1,0:T(8,128)S(1)} %copy-done.15), channel_id=1, source_target_pairs={{0,1},{1,2},{2,3},{3,0},{4,5},{5,6},{6,7},{7,4},{8,9},{9,10},{10,1... | collective-permute-start | bytes 393224 | tf_op jit(solution)/shard_map/ppermute | solution.py:323
  77.0 21.7 %collective-permute-start.1 = (f32[2,128,128]{2,1,0:T(8,128)S(1)}, f32[2,128,128]{2,1,0:T(8,128)S(1)}, u32[]{:S(2)}, u32[]{:S(2)}) collective-permute-start(f32[2,128,128]{2,1,0:T(8,128)S(1)} %copy-done.14), channel_id=1, source_target_pairs={{0,3},{1,0},{2,1},{3,2},{4,7},{5,4},{6,5},{7,6},{8,11},{9,8},{10,9... | collective-permute-start | bytes 393224 | tf_op jit(solution)/shard_map/ppermute | solution.py:323
  78.1 15.7 %copy-start.7 = (f32[6,128,128]{2,1,0:T(8,128)S(1)}, f32[6,128,128]{2,1,0:T(8,128)}, u32[]{:S(2)}) copy-start(f32[6,128,128]{2,1,0:T(8,128)} %get-tuple-element.37.refs_0_) | copy-start | bytes 1179652
  87.1 12.2 %collective-permute-start.2 = (f32[2,128,128]{2,1,0:T(8,128)S(1)}, f32[2,128,128]{2,1,0:T(8,128)S(1)}, u32[]{:S(2)}, u32[]{:S(2)}) collective-permute-start(f32[2,128,128]{2,1,0:T(8,128)S(1)} %copy-done.13), channel_id=1, source_target_pairs={{0,2},{1,3},{2,0},{3,1},{4,6},{5,7},{6,4},{7,5},{8,10},{9,11},{10,... | collective-permute-start | bytes 393224 | tf_op jit(solution)/shard_map/ppermute | solution.py:323
  102.4 3.3 %collective-permute-start.15 = (f32[640,128]{1,0:T(8,128)S(1)}, f32[640,128]{1,0:T(8,128)S(1)}, u32[]{:S(2)}, u32[]{:S(2)}) collective-permute-start(f32[640,128]{1,0:T(8,128)S(1)} %get-tuple-element.62), channel_id=1, source_target_pairs={{0,4},{4,0},{1,5},{5,1},{2,6},{6,2},{3,7},{7,3},{8,12},{12,8},{9,1... | collective-permute-start | bytes 983048 | tf_op jit(solution)/shard_map/ppermute | solution.py:191
  122.1 2.7 %collective-permute-start.16 = (f32[40,128]{1,0:T(8,128)S(1)}, f32[40,128]{1,0:T(8,128)S(1)}, u32[]{:S(2)}, u32[]{:S(2)}) collective-permute-start(f32[40,128]{1,0:T(8,128)S(1)} %reduce_sum.9), channel_id=1, source_target_pairs={{0,1},{1,0},{2,3},{3,2},{4,5},{5,4},{6,7},{7,6},{8,9},{9,8},{10,11... | collective-permute-start | bytes 61448 | tf_op jit(solution)/shard_map/ppermute | solution.py:197
  124.8 3.8 %collective-permute-start.17 = (f32[40,128]{1,0:T(8,128)S(1)}, f32[40,128]{1,0:T(8,128)S(1)}, u32[]{:S(2)}, u32[]{:S(2)}) collective-permute-start(f32[40,128]{1,0:T(8,128)S(1)} %add.10), channel_id=1, source_target_pairs={{0,3},{1,2},{2,1},{3,0},{4,7},{5,6},{6,5},{7,4},{8,11},{9,10},{10,... | collective-permute-start | bytes 61448 | tf_op jit(solution)/shard_map/ppermute | solution.py:197
  139.4 6.3 %collective-permute-start.18 = (f32[640,128]{1,0:T(8,128)S(1)}, f32[640,128]{1,0:T(8,128)S(1)}, u32[]{:S(2)}, u32[]{:S(2)}) collective-permute-start(f32[640,128]{1,0:T(8,128)S(1)} %bitcast.19), channel_id=1, source_target_pairs={{0,4},{4,0},{1,5},{5,1},{2,6},{6,2},{3,7},{7,3},{8,12},{12,8},{9,1... | collective-permute-start | bytes 983048 | tf_op jit(solution)/shard_map/ppermute | solution.py:199
  (11 other events, 63.0 us)

commit v3 on v2

--- a/solution.py
+++ b/solution.py
@@ -47,11 +47,11 @@
 
 
 def pack(slab, comp, ranges):
-    rows = 1024
+    rows = 2048
     shapes = [(d, 128, 128) for _, d in ranges for _ in range(4)]
     outs = pl.pallas_call(
         functools.partial(pack_kernel, ranges),
-        grid=(2,),
+        grid=(1,),
         in_specs=[
             pl.BlockSpec((None, rows, 128), lambda i: (comp, i, 0)),
             pl.BlockSpec((None, rows, 128), lambda i: (comp, i, 1)),

time: 161 us -> 161 us (level)
  no operation moved by 1% of the time
where the time goes in v3:
time: 161 us
  Pallas kernels  55.1 us (34%)
  waiting for transfers between devices  46.6 us (29%)
  starting transfers between devices  28.6 us (18%)
  blocking collectives  27.1 us (17%)
  local copies, waits for them, and re-layouts  2.68 us (2%)
    ppermute x15, waiting for transfers between devices, on_device(): arrived.append([lax.ppermute(p[k], 'narrow', ring(4, k)) for k in SHIFTS])  40.9 us
    all_to_all x2, blocking collectives, total(): deal = lambda x, axes: lax.all_to_all(x, axes, 0, 0, tiled=True)  27.1 us
    pallas_call x5, Pallas kernels, gram_step(): pl.pallas_call(functools.partial(gram_kernel, first, last, merge, base),...  24 us
    ppermute x15, starting transfers between devices, on_device(): arrived.append([lax.ppermute(p[k], 'narrow', ring(4, k)) for k in SHIFTS])  18.2 us
    pallas_call x4, Pallas kernels, pack(): pl.pallas_call(functools.partial(pack_kernel, ranges), grid=(1,), in_spec...  16.9 us
    pallas_call x1, Pallas kernels, upper_factor(): pl.pallas_call(functools.partial(chol_kernel, scale), out_shape=jax.Shape...  14.2 us
    ppermute x1, starting transfers between devices, total(): return (h, lax.ppermute(h, 'core', swap))  5.03 us
    ppermute x2, starting transfers between devices, total(): piece += lax.ppermute(piece, 'narrow', [(i, i ^ flip) for i in range(4)])  3.36 us
  transfers between devices with their start and end apart: 19, of which 12 were waited for; matrix products, arithmetic and copies ran while one was open for 0% of the time, Pallas kernels for 21%

profile of v3, /device:TPU:1, one launch (start us, length us, event | category | flops | bytes accessed | tf_op | source)
XLA Modules:
  0.0 160.8 jit_solution(881924056959203439)
XLA Ops:
  0.6 4.2 %pack.7 = (f32[8,128,128]{2,1,0:T(8,128)}, f32[8,128,128]{2,1,0:T(8,128)}, f32[8,128,128]{2,1,0:T(8,128)}, f32[8,128,128]{2,1,0:T(8,128)}) custom-call(f32[4,2048,256]{2,1,0:T(8,128)} %bitcast.10, f32[4,2048,256]{2,1,0:T(8,128)} %bitcast.11), custom_call_target="tpu_custom_call" | custom-call | flops 1048576 | bytes 4194304 | tf_op jit(solution)/shard_map/pack/pallas_call | solution.py:52
  4.8 2.0 %collective-permute-start.12 = (f32[8,128,128]{2,1,0:T(8,128)}, f32[8,128,128]{2,1,0:T(8,128)S(1)}, u32[]{:S(2)}, u32[]{:S(2)}) collective-permute-start(f32[8,128,128]{2,1,0:T(8,128)} %get-tuple-element.50), channel_id=1, source_target_pairs={{0,1},{1,2},{2,3},{3,0},{4,5},{5,6},{6,7},{7,4},{8,9},{9,10},{10,1... | collective-permute-start | bytes 1572872 | tf_op jit(solution)/shard_map/ppermute | solution.py:323
  9.9 4.2 %pack.6 = (f32[8,128,128]{2,1,0:T(8,128)}, f32[8,128,128]{2,1,0:T(8,128)}, f32[8,128,128]{2,1,0:T(8,128)}, f32[8,128,128]{2,1,0:T(8,128)}) custom-call(f32[4,2048,256]{2,1,0:T(8,128)} %bitcast.12, f32[4,2048,256]{2,1,0:T(8,128)} %bitcast.13), custom_call_target="tpu_custom_call" | custom-call | flops 1048576 | bytes 4194304 | tf_op jit(solution)/shard_map/pack/pallas_call | solution.py:52
  16.2 4.2 %pack.5 = (f32[8,128,128]{2,1,0:T(8,128)}, f32[8,128,128]{2,1,0:T(8,128)}, f32[8,128,128]{2,1,0:T(8,128)}, f32[8,128,128]{2,1,0:T(8,128)}) custom-call(f32[4,2048,256]{2,1,0:T(8,128)} %bitcast.14, f32[4,2048,256]{2,1,0:T(8,128)} %bitcast.15), custom_call_target="tpu_custom_call" | custom-call | flops 1048576 | bytes 4194304 | tf_op jit(solution)/shard_map/pack/pallas_call | solution.py:52
  22.6 4.2 %pack.4 = (f32[6,128,128]{2,1,0:T(8,128)}, f32[6,128,128]{2,1,0:T(8,128)}, f32[6,128,128]{2,1,0:T(8,128)}, f32[6,128,128]{2,1,0:T(8,128)}, f32[2,128,128]{2,1,0:...) custom-call(f32[4,2048,256]{2,1,0:T(8,128)} %bitcast.16, f32[4,2048,256]{2,1,0:T(8,128)} %bitcast.17), custom_call_target="tpu_custom_call" | custom-call | flops 1048576 | bytes 4194304 | tf_op jit(solution)/shard_map/pack/pallas_call | solution.py:52
  26.9 5.4 %collective-permute-done.14.refs_3_ = f32[8,128,128]{2,1,0:T(8,128)} collective-permute-done((f32[8,128,128]{2,1,0:T(8,128)}, f32[8,128,128]{2,1,0:T(8,128)}, u32[]{:S(2)}, u32[]{:S(2)}) %collective-permute-start.14) | collective-permute-done | bytes 524320 | tf_op jit(solution)/shard_map/ppermute | solution.py:323
  33.3 8.7 %collective-permute-done.10.refs_2_ = f32[8,128,128]{2,1,0:T(8,128)S(1)} collective-permute-done((f32[8,128,128]{2,1,0:T(8,128)}, f32[8,128,128]{2,1,0:T(8,128)S(1)}, u32[]{:S(2)}, u32[]{:S(2)}) %collective-permute-start.10) | collective-permute-done | bytes 524320 | tf_op jit(solution)/shard_map/ppermute | solution.py:323
  42.1 2.4 %collective-permute-start.8 = (f32[8,128,128]{2,1,0:T(8,128)}, f32[8,128,128]{2,1,0:T(8,128)S(1)}, u32[]{:S(2)}, u32[]{:S(2)}) collective-permute-start(f32[8,128,128]{2,1,0:T(8,128)} %get-tuple-element.44), channel_id=1, source_target_pairs={{0,2},{1,3},{2,0},{3,1},{4,6},{5,7},{6,4},{7,5},{8,10},{9,11},{10,... | collective-permute-start | bytes 1572872 | tf_op jit(solution)/shard_map/ppermute | solution.py:323
  45.6 6.1 %gram.5 = (f32[1280,128]{1,0:T(8,128)S(1)}, f32[4,1024,64]{2,1,0:T(8,128)}) custom-call(f32[8,128,128]{2,1,0:T(8,128)S(1)} %copy-done.4, f32[8,128,128]{2,1,0:T(8,128)S(1)} %collective-permute-done.12.refs_1_, f32[8,128,128]{2,1,0:T(8,128)S(1)} %copy-done.6, f32[8,128,128]{2,1,0:T(8,128)} %collective-permute-done.14.refs_3_, f32[64,512]{1,0:T(8,128)S(1)} %bitcast.5), custom_call_target="tpu_custom_call" | custom-call | flops 3221225472 | bytes 4194304 | tf_op jit(solution)/shard_map/gram/pallas_call | solution.py:171
  51.7 3.5 %collective-permute-start.3 = (f32[6,128,128]{2,1,0:T(8,128)S(1)}, f32[6,128,128]{2,1,0:T(8,128)S(1)}, u32[]{:S(2)}, u32[]{:S(2)}) collective-permute-start(f32[6,128,128]{2,1,0:T(8,128)S(1)} %copy-done.12), channel_id=1, source_target_pairs={{0,1},{1,2},{2,3},{3,0},{4,5},{5,6},{6,7},{7,4},{8,9},{9,10},{10,1... | collective-permute-start | bytes 1179656 | tf_op jit(solution)/shard_map/ppermute | solution.py:323
  55.8 12.0 %collective-permute-done.6.refs_1_ = f32[8,128,128]{2,1,0:T(8,128)S(1)} collective-permute-done((f32[8,128,128]{2,1,0:T(8,128)}, f32[8,128,128]{2,1,0:T(8,128)S(1)}, u32[]{:S(2)}, u32[]{:S(2)}) %collective-permute-start.6) | collective-permute-done | bytes 524320 | tf_op jit(solution)/shard_map/ppermute | solution.py:323
  68.5 5.1 %gram.6 = (f32[1280,128]{1,0:T(8,128)S(1)}, f32[4,1024,64]{2,1,0:T(8,128)}) custom-call(f32[8,128,128]{2,1,0:T(8,128)S(1)} %copy-done.3, f32[8,128,128]{2,1,0:T(8,128)S(1)} %collective-permute-done.9.refs_1_, f32[8,128,128]{2,1,0:T(8,128)S(1)} %collective-permute-done.10.refs_2_, ...), custom_call_target="tpu_custom_call", output_to_operand_aliasing={{0}: (5, {}), {1}: (6, {})} | custom-call | flops 3221225472 | bytes 4194304 | tf_op jit(solution)/shard_map/gram/pallas_call | solution.py:171
  73.6 3.6 %collective-permute-done.8.refs_3_ = f32[8,128,128]{2,1,0:T(8,128)S(1)} collective-permute-done((f32[8,128,128]{2,1,0:T(8,128)}, f32[8,128,128]{2,1,0:T(8,128)S(1)}, u32[]{:S(2)}, u32[]{:S(2)}) %collective-permute-start.8) | collective-permute-done | bytes 524320 | tf_op jit(solution)/shard_map/ppermute | solution.py:323
  78.3 5.0 %gram.7 = (f32[1280,128]{1,0:T(8,128)S(1)}, f32[4,1024,64]{2,1,0:T(8,128)}) custom-call(f32[8,128,128]{2,1,0:T(8,128)S(1)} %copy-done.2, f32[8,128,128]{2,1,0:T(8,128)S(1)} %collective-permute-done.6.refs_1_, f32[8,128,128]{2,1,0:T(8,128)S(1)} %collective-permute-done.7.refs_2_, ...), custom_call_target="tpu_custom_call", output_to_operand_aliasing={{0}: (5, {}), {1}: (6, {})} | custom-call | flops 3221225472 | bytes 4194304 | tf_op jit(solution)/shard_map/gram/pallas_call | solution.py:171
  83.3 4.0 %collective-permute-done.3.refs_1_ = f32[6,128,128]{2,1,0:T(8,128)S(1)} collective-permute-done((f32[6,128,128]{2,1,0:T(8,128)S(1)}, f32[6,128,128]{2,1,0:T(8,128)S(1)}, u32[]{:S(2)}, u32[]{:S(2)}) %collective-permute-start.3) | collective-permute-done | bytes 393248 | tf_op jit(solution)/shard_map/ppermute | solution.py:323
  87.9 6.1 %collective-permute-done.5.refs_3_ = f32[6,128,128]{2,1,0:T(8,128)S(1)} collective-permute-done((f32[6,128,128]{2,1,0:T(8,128)S(1)}, f32[6,128,128]{2,1,0:T(8,128)S(1)}, u32[]{:S(2)}, u32[]{:S(2)}) %collective-permute-start.5) | collective-permute-done | bytes 393248 | tf_op jit(solution)/shard_map/ppermute | solution.py:323
  94.0 4.8 %gram.8 = (f32[1280,128]{1,0:T(8,128)S(1)}, f32[4,1024,64]{2,1,0:T(8,128)}) custom-call(f32[6,128,128]{2,1,0:T(8,128)S(1)} %copy-done.7, f32[6,128,128]{2,1,0:T(8,128)S(1)} %collective-permute-done.3.refs_1_, f32[6,128,128]{2,1,0:T(8,128)S(1)} %collective-permute-done.4.refs_2_, ...), custom_call_target="tpu_custom_call", output_to_operand_aliasing={{0}: (5, {}), {1}: (6, {})} | custom-call | flops 2415919104 | bytes 3145728 | tf_op jit(solution)/shard_map/gram/pallas_call | solution.py:171
  99.5 3.1 %gram.9 = (f32[640,128]{1,0:T(8,128)S(1)}, f32[640,128]{1,0:T(8,128)S(1)}, f32[4,1024,64]{2,1,0:T(8,128)}) custom-call(f32[2,128,128]{2,1,0:T(8,128)S(1)} %copy-done.1, f32[2,128,128]{2,1,0:T(8,128)S(1)} %collective-permute-done.refs_1_, f32[2,128,128]{2,1,0:T(8,128)S(1)} %collective-permute-done.1.refs_2_, ...), custom_call_target="tpu_custom_call", output_to_operand_aliasing={{2}: (6, {})} | custom-call | flops 805306368 | bytes 1048576 | tf_op jit(solution)/shard_map/gram/pallas_call | solution.py:171
  102.5 2.0 %collective-permute-start.15 = (f32[640,128]{1,0:T(8,128)S(1)}, f32[640,128]{1,0:T(8,128)S(1)}, u32[]{:S(2)}, u32[]{:S(2)}) collective-permute-start(f32[640,128]{1,0:T(8,128)S(1)} %get-tuple-element.62), channel_id=1, source_target_pairs={{0,4},{4,0},{1,5},{5,1},{2,6},{6,2},{3,7},{7,3},{8,12},{12,8},{9,1... | collective-permute-start | bytes 983048 | tf_op jit(solution)/shard_map/ppermute | solution.py:191
  105.9 16.4 %all_to_all.10 = f32[16,40,128]{2,1,0:T(8,128)S(1)} all-to-all(f32[16,40,128]{2,1,0:T(8,128)S(1)} %bitcast.21), channel_id=1, replica_groups=mesh['z'=4,'y'=4,'core'=2,'narrow'=4] {'z','y'}, dimensions={0} | all-to-all | bytes 655360 | tf_op jit(solution)/shard_map/all_to_all | solution.py:193
  125.0 2.0 %collective-permute-start.17 = (f32[40,128]{1,0:T(8,128)S(1)}, f32[40,128]{1,0:T(8,128)S(1)}, u32[]{:S(2)}, u32[]{:S(2)}) collective-permute-start(f32[40,128]{1,0:T(8,128)S(1)} %add.10), channel_id=1, source_target_pairs={{0,3},{1,2},{2,1},{3,0},{4,7},{5,6},{6,5},{7,4},{8,11},{9,10},{10,... | collective-permute-start | bytes 61448 | tf_op jit(solution)/shard_map/ppermute | solution.py:197
  128.9 10.7 %all_to_all.11 = f32[16,40,128]{2,1,0:T(8,128)S(1)} all-to-all(f32[16,40,128]{2,1,0:T(8,128)S(1)} %broadcast_in_dim.2), channel_id=1, replica_groups=mesh['z'=4,'y'=4,'core'=2,'narrow'=4] {'z','y'}, dimensions={0} | all-to-all | bytes 655360 | tf_op jit(solution)/shard_map/all_to_all | solution.py:193
  139.6 5.0 %collective-permute-start.18 = (f32[640,128]{1,0:T(8,128)S(1)}, f32[640,128]{1,0:T(8,128)S(1)}, u32[]{:S(2)}, u32[]{:S(2)}) collective-permute-start(f32[640,128]{1,0:T(8,128)S(1)} %bitcast.19), channel_id=1, source_target_pairs={{0,4},{4,0},{1,5},{5,1},{2,6},{6,2},{3,7},{7,3},{8,12},{12,8},{9,1... | collective-permute-start | bytes 983048 | tf_op jit(solution)/shard_map/ppermute | solution.py:199
  146.6 14.2 %upper_factor.1 = f32[512,512]{1,0:T(8,128)} custom-call(f32[640,128]{1,0:T(8,128)} %bitcast.20, f32[640,128]{1,0:T(8,128)} %copy-done.9), custom_call_target="tpu_custom_call" | custom-call | tf_op jit(solution)/shard_map/upper_factor/pallas_call | solution.py:301
  (63 shorter events, 21.1 us)
Async XLA Ops:
  4.8 15.6 %collective-permute-start.12 = (f32[8,128,128]{2,1,0:T(8,128)}, f32[8,128,128]{2,1,0:T(8,128)S(1)}, u32[]{:S(2)}, u32[]{:S(2)}) collective-permute-start(f32[8,128,128]{2,1,0:T(8,128)} %get-tuple-element.50), channel_id=1, source_target_pairs={{0,1},{1,2},{2,3},{3,0},{4,5},{5,6},{6,7},{7,4},{8,9},{9,10},{10,1... | collective-permute-start | bytes 1572872 | tf_op jit(solution)/shard_map/ppermute | solution.py:323
  6.9 13.5 %collective-permute-start.13 = (f32[8,128,128]{2,1,0:T(8,128)}, f32[8,128,128]{2,1,0:T(8,128)S(1)}, u32[]{:S(2)}, u32[]{:S(2)}) collective-permute-start(f32[8,128,128]{2,1,0:T(8,128)} %get-tuple-element.51), channel_id=1, source_target_pairs={{0,3},{1,0},{2,1},{3,2},{4,7},{5,4},{6,5},{7,6},{8,11},{9,8},{10,9... | collective-permute-start | bytes 1572872 | tf_op jit(solution)/shard_map/ppermute | solution.py:323
  8.1 24.1 %collective-permute-start.14 = (f32[8,128,128]{2,1,0:T(8,128)}, f32[8,128,128]{2,1,0:T(8,128)}, u32[]{:S(2)}, u32[]{:S(2)}) collective-permute-start(f32[8,128,128]{2,1,0:T(8,128)} %get-tuple-element.52), channel_id=1, source_target_pairs={{0,2},{1,3},{2,0},{3,1},{4,6},{5,7},{6,4},{7,5},{8,10},{9,11},{10,... | collective-permute-start | bytes 1572872 | tf_op jit(solution)/shard_map/ppermute | solution.py:323
  14.1 28.0 %collective-permute-start.10 = (f32[8,128,128]{2,1,0:T(8,128)}, f32[8,128,128]{2,1,0:T(8,128)S(1)}, u32[]{:S(2)}, u32[]{:S(2)}) collective-permute-start(f32[8,128,128]{2,1,0:T(8,128)} %get-tuple-element.47), channel_id=1, source_target_pairs={{0,3},{1,0},{2,1},{3,2},{4,7},{5,4},{6,5},{7,6},{8,11},{9,8},{10,9... | collective-permute-start | bytes 1572872 | tf_op jit(solution)/shard_map/ppermute | solution.py:323
  15.0 36.7 %collective-permute-start.11 = (f32[8,128,128]{2,1,0:T(8,128)}, f32[8,128,128]{2,1,0:T(8,128)S(1)}, u32[]{:S(2)}, u32[]{:S(2)}) collective-permute-start(f32[8,128,128]{2,1,0:T(8,128)} %get-tuple-element.48), channel_id=1, source_target_pairs={{0,2},{1,3},{2,0},{3,1},{4,6},{5,7},{6,4},{7,5},{8,10},{9,11},{10,... | collective-permute-start | bytes 1572872 | tf_op jit(solution)/shard_map/ppermute | solution.py:323
  20.4 35.2 %collective-permute-start.9 = (f32[8,128,128]{2,1,0:T(8,128)}, f32[8,128,128]{2,1,0:T(8,128)S(1)}, u32[]{:S(2)}, u32[]{:S(2)}) collective-permute-start(f32[8,128,128]{2,1,0:T(8,128)} %get-tuple-element.46), channel_id=1, source_target_pairs={{0,1},{1,2},{2,3},{3,0},{4,5},{5,6},{6,7},{7,4},{8,9},{9,10},{10,1... | collective-permute-start | bytes 1572872 | tf_op jit(solution)/shard_map/ppermute | solution.py:323
  21.3 23.3 %copy-start = (f32[512,64]{0,1:T(8,128)S(1)}, f32[512,64]{0,1:T(8,128)}, u32[]{:S(2)}) copy-start(f32[512,64]{0,1:T(8,128)} %param.3) | copy-start | bytes 393220
  21.3 23.3 %copy-start.4 = (f32[8,128,128]{2,1,0:T(8,128)S(1)}, f32[8,128,128]{2,1,0:T(8,128)}, u32[]{:S(2)}) copy-start(f32[8,128,128]{2,1,0:T(8,128)} %get-tuple-element.49.refs_0_) | copy-start | bytes 1572868
  21.3 46.6 %collective-permute-start.6 = (f32[8,128,128]{2,1,0:T(8,128)}, f32[8,128,128]{2,1,0:T(8,128)S(1)}, u32[]{:S(2)}, u32[]{:S(2)}) collective-permute-start(f32[8,128,128]{2,1,0:T(8,128)} %get-tuple-element.42), channel_id=1, source_target_pairs={{0,1},{1,2},{2,3},{3,0},{4,5},{5,6},{6,7},{7,4},{8,9},{9,10},{10,1... | collective-permute-start | bytes 1572872 | tf_op jit(solution)/shard_map/ppermute | solution.py:323
  32.2 41.3 %collective-permute-start.7 = (f32[8,128,128]{2,1,0:T(8,128)}, f32[8,128,128]{2,1,0:T(8,128)S(1)}, u32[]{:S(2)}, u32[]{:S(2)}) collective-permute-start(f32[8,128,128]{2,1,0:T(8,128)} %get-tuple-element.43), channel_id=1, source_target_pairs={{0,3},{1,0},{2,1},{3,2},{4,7},{5,4},{6,5},{7,6},{8,11},{9,8},{10,9... | collective-permute-start | bytes 1572872 | tf_op jit(solution)/shard_map/ppermute | solution.py:323
  42.1 35.0 %collective-permute-start.8 = (f32[8,128,128]{2,1,0:T(8,128)}, f32[8,128,128]{2,1,0:T(8,128)S(1)}, u32[]{:S(2)}, u32[]{:S(2)}) collective-permute-start(f32[8,128,128]{2,1,0:T(8,128)} %get-tuple-element.44), channel_id=1, source_target_pairs={{0,2},{1,3},{2,0},{3,1},{4,6},{5,7},{6,4},{7,5},{8,10},{9,11},{10,... | collective-permute-start | bytes 1572872 | tf_op jit(solution)/shard_map/ppermute | solution.py:323
  45.6 22.3 %copy-start.10 = (f32[6,128,128]{2,1,0:T(8,128)S(1)}, f32[6,128,128]{2,1,0:T(8,128)}, u32[]{:S(2)}) copy-start(f32[6,128,128]{2,1,0:T(8,128)} %get-tuple-element.40) | copy-start | bytes 1179652
  45.6 22.9 %copy-start.3 = (f32[8,128,128]{2,1,0:T(8,128)S(1)}, f32[8,128,128]{2,1,0:T(8,128)}, u32[]{:S(2)}) copy-start(f32[8,128,128]{2,1,0:T(8,128)} %get-tuple-element.45.refs_0_) | copy-start | bytes 1572868
  51.7 35.6 %collective-permute-start.3 = (f32[6,128,128]{2,1,0:T(8,128)S(1)}, f32[6,128,128]{2,1,0:T(8,128)S(1)}, u32[]{:S(2)}, u32[]{:S(2)}) collective-permute-start(f32[6,128,128]{2,1,0:T(8,128)S(1)} %copy-done.12), channel_id=1, source_target_pairs={{0,1},{1,2},{2,3},{3,0},{4,5},{5,6},{6,7},{7,4},{8,9},{9,10},{10,1... | collective-permute-start | bytes 1179656 | tf_op jit(solution)/shard_map/ppermute | solution.py:323
  55.6 32.3 %collective-permute-start.4 = (f32[6,128,128]{2,1,0:T(8,128)S(1)}, f32[6,128,128]{2,1,0:T(8,128)S(1)}, u32[]{:S(2)}, u32[]{:S(2)}) collective-permute-start(f32[6,128,128]{2,1,0:T(8,128)S(1)} %copy-done.11), channel_id=1, source_target_pairs={{0,3},{1,0},{2,1},{3,2},{4,7},{5,4},{6,5},{7,6},{8,11},{9,8},{10,9... | collective-permute-start | bytes 1179656 | tf_op jit(solution)/shard_map/ppermute | solution.py:323
  67.9 26.2 %collective-permute-start.5 = (f32[6,128,128]{2,1,0:T(8,128)S(1)}, f32[6,128,128]{2,1,0:T(8,128)S(1)}, u32[]{:S(2)}, u32[]{:S(2)}) collective-permute-start(f32[6,128,128]{2,1,0:T(8,128)S(1)} %copy-done.10), channel_id=1, source_target_pairs={{0,2},{1,3},{2,0},{3,1},{4,6},{5,7},{6,4},{7,5},{8,10},{9,11},{10,... | collective-permute-start | bytes 1179656 | tf_op jit(solution)/shard_map/ppermute | solution.py:323
  73.6 25.2 %collective-permute-start = (f32[2,128,128]{2,1,0:T(8,128)S(1)}, f32[2,128,128]{2,1,0:T(8,128)S(1)}, u32[]{:S(2)}, u32[]{:S(2)}) collective-permute-start(f32[2,128,128]{2,1,0:T(8,128)S(1)} %copy-done.15), channel_id=1, source_target_pairs={{0,1},{1,2},{2,3},{3,0},{4,5},{5,6},{6,7},{7,4},{8,9},{9,10},{10,1... | collective-permute-start | bytes 393224 | tf_op jit(solution)/shard_map/ppermute | solution.py:323
  77.1 21.7 %collective-permute-start.1 = (f32[2,128,128]{2,1,0:T(8,128)S(1)}, f32[2,128,128]{2,1,0:T(8,128)S(1)}, u32[]{:S(2)}, u32[]{:S(2)}) collective-permute-start(f32[2,128,128]{2,1,0:T(8,128)S(1)} %copy-done.14), channel_id=1, source_target_pairs={{0,3},{1,0},{2,1},{3,2},{4,7},{5,4},{6,5},{7,6},{8,11},{9,8},{10,9... | collective-permute-start | bytes 393224 | tf_op jit(solution)/shard_map/ppermute | solution.py:323
  78.3 15.7 %copy-start.7 = (f32[6,128,128]{2,1,0:T(8,128)S(1)}, f32[6,128,128]{2,1,0:T(8,128)}, u32[]{:S(2)}) copy-start(f32[6,128,128]{2,1,0:T(8,128)} %get-tuple-element.37.refs_0_) | copy-start | bytes 1179652
  87.3 12.2 %collective-permute-start.2 = (f32[2,128,128]{2,1,0:T(8,128)S(1)}, f32[2,128,128]{2,1,0:T(8,128)S(1)}, u32[]{:S(2)}, u32[]{:S(2)}) collective-permute-start(f32[2,128,128]{2,1,0:T(8,128)S(1)} %copy-done.13), channel_id=1, source_target_pairs={{0,2},{1,3},{2,0},{3,1},{4,6},{5,7},{6,4},{7,5},{8,10},{9,11},{10,... | collective-permute-start | bytes 393224 | tf_op jit(solution)/shard_map/ppermute | solution.py:323
  102.5 3.3 %collective-permute-start.15 = (f32[640,128]{1,0:T(8,128)S(1)}, f32[640,128]{1,0:T(8,128)S(1)}, u32[]{:S(2)}, u32[]{:S(2)}) collective-permute-start(f32[640,128]{1,0:T(8,128)S(1)} %get-tuple-element.62), channel_id=1, source_target_pairs={{0,4},{4,0},{1,5},{5,1},{2,6},{6,2},{3,7},{7,3},{8,12},{12,8},{9,1... | collective-permute-start | bytes 983048 | tf_op jit(solution)/shard_map/ppermute | solution.py:191
  122.3 2.7 %collective-permute-start.16 = (f32[40,128]{1,0:T(8,128)S(1)}, f32[40,128]{1,0:T(8,128)S(1)}, u32[]{:S(2)}, u32[]{:S(2)}) collective-permute-start(f32[40,128]{1,0:T(8,128)S(1)} %reduce_sum.9), channel_id=1, source_target_pairs={{0,1},{1,0},{2,3},{3,2},{4,5},{5,4},{6,7},{7,6},{8,9},{9,8},{10,11... | collective-permute-start | bytes 61448 | tf_op jit(solution)/shard_map/ppermute | solution.py:197
  125.0 3.8 %collective-permute-start.17 = (f32[40,128]{1,0:T(8,128)S(1)}, f32[40,128]{1,0:T(8,128)S(1)}, u32[]{:S(2)}, u32[]{:S(2)}) collective-permute-start(f32[40,128]{1,0:T(8,128)S(1)} %add.10), channel_id=1, source_target_pairs={{0,3},{1,2},{2,1},{3,0},{4,7},{5,6},{6,5},{7,4},{8,11},{9,10},{10,... | collective-permute-start | bytes 61448 | tf_op jit(solution)/shard_map/ppermute | solution.py:197
  139.6 6.3 %collective-permute-start.18 = (f32[640,128]{1,0:T(8,128)S(1)}, f32[640,128]{1,0:T(8,128)S(1)}, u32[]{:S(2)}, u32[]{:S(2)}) collective-permute-start(f32[640,128]{1,0:T(8,128)S(1)} %bitcast.19), channel_id=1, source_target_pairs={{0,4},{4,0},{1,5},{5,1},{2,6},{6,2},{3,7},{7,3},{8,12},{12,8},{9,1... | collective-permute-start | bytes 983048 | tf_op jit(solution)/shard_map/ppermute | solution.py:199
  (11 other events, 63.0 us)

commit v4 on v3

--- a/solution.py
+++ b/solution.py
@@ -272,10 +272,18 @@
                 work[t, base + 8 * last:base + 128, :] -= part[8 * last:, o:o + 128]
 
 
-def chol_kernel(scale, mine_ref, other_ref, out_ref, gram, work):
+def chol_kernel(scale, mine_ref, other_ref, out_ref, gram, work, sems):
     c = lax.axis_index("core")
-    gram[pl.ds(pl.multiple_of(c * HALF, 128), HALF), :] = mine_ref[...]
-    gram[pl.ds(pl.multiple_of((1 - c) * HALF, 128), HALF), :] = other_ref[...]
+    copies = [
+        pltpu.make_async_copy(
+            ref, gram.at[pl.ds(pl.multiple_of(at * HALF, 128), HALF), :], sems.at[k]
+        )
+        for k, (ref, at) in enumerate(((mine_ref, c), (other_ref, 1 - c)))
+    ]
+    for copy in copies:
+        copy.start()
+    for copy in copies:
+        copy.wait()
     for k, (i, j) in enumerate(BLOCKS):
         work[j, i * 128:(i + 1) * 128, :] = gram[k * 128:(k + 1) * 128, :] * scale
     for b in range(4):
@@ -301,9 +309,13 @@
     return pl.pallas_call(
         functools.partial(chol_kernel, scale),
         out_shape=jax.ShapeDtypeStruct((512, 512), F32),
-        in_specs=[pl.BlockSpec((HALF, 128), lambda: (0, 0))] * 2,
+        in_specs=[pl.BlockSpec(memory_space=pl.ANY)] * 2,
         out_specs=pl.BlockSpec((512, 512), lambda: (0, 0)),
-        scratch_shapes=[pltpu.VMEM((1280, 128), F32), pltpu.VMEM((4, 512, 128), F32)],
+        scratch_shapes=[
+            pltpu.VMEM((1280, 128), F32),
+            pltpu.VMEM((4, 512, 128), F32),
+            pltpu.SemaphoreType.DMA((2,)),
+        ],
         name="upper_factor",
     )(mine, other)
 

time: 161 us -> 161 us (level)
  no operation moved by 1% of the time
where the time goes in v4:
time: 161 us
  Pallas kernels  55.1 us (34%)
  waiting for transfers between devices  46.6 us (29%)
  starting transfers between devices  28.6 us (18%)
  blocking collectives  27.1 us (17%)
  local copies, waits for them, and re-layouts  2.68 us (2%)
    ppermute x15, waiting for transfers between devices, on_device(): arrived.append([lax.ppermute(p[k], 'narrow', ring(4, k)) for k in SHIFTS])  40.9 us
    all_to_all x2, blocking collectives, total(): deal = lambda x, axes: lax.all_to_all(x, axes, 0, 0, tiled=True)  27.1 us
    pallas_call x5, Pallas kernels, gram_step(): pl.pallas_call(functools.partial(gram_kernel, first, last, merge, base),...  24 us
    ppermute x15, starting transfers between devices, on_device(): arrived.append([lax.ppermute(p[k], 'narrow', ring(4, k)) for k in SHIFTS])  18.2 us
    pallas_call x4, Pallas kernels, pack(): pl.pallas_call(functools.partial(pack_kernel, ranges), grid=(1,), in_spec...  16.9 us
    pallas_call x1, Pallas kernels, upper_factor(): pl.pallas_call(functools.partial(chol_kernel, scale), out_shape=jax.Shape...  14.2 us
    ppermute x1, starting transfers between devices, total(): return (h, lax.ppermute(h, 'core', swap))  5.03 us
    ppermute x2, starting transfers between devices, total(): piece += lax.ppermute(piece, 'narrow', [(i, i ^ flip) for i in range(4)])  3.36 us
  transfers between devices with their start and end apart: 19, of which 12 were waited for; matrix products, arithmetic and copies ran while one was open for 0% of the time, Pallas kernels for 21%

profile of v4, /device:TPU:1, one launch (start us, length us, event | category | flops | bytes accessed | tf_op | source)
XLA Modules:
  0.0 161.0 jit_solution(9536788095157246949)
XLA Ops:
  0.6 4.2 %pack.7 = (f32[8,128,128]{2,1,0:T(8,128)}, f32[8,128,128]{2,1,0:T(8,128)}, f32[8,128,128]{2,1,0:T(8,128)}, f32[8,128,128]{2,1,0:T(8,128)}) custom-call(f32[4,2048,256]{2,1,0:T(8,128)} %bitcast.10, f32[4,2048,256]{2,1,0:T(8,128)} %bitcast.11), custom_call_target="tpu_custom_call" | custom-call | flops 1048576 | bytes 4194304 | tf_op jit(solution)/shard_map/pack/pallas_call | solution.py:52
  4.8 2.0 %collective-permute-start.12 = (f32[8,128,128]{2,1,0:T(8,128)}, f32[8,128,128]{2,1,0:T(8,128)S(1)}, u32[]{:S(2)}, u32[]{:S(2)}) collective-permute-start(f32[8,128,128]{2,1,0:T(8,128)} %get-tuple-element.50), channel_id=1, source_target_pairs={{0,1},{1,2},{2,3},{3,0},{4,5},{5,6},{6,7},{7,4},{8,9},{9,10},{10,1... | collective-permute-start | bytes 1572872 | tf_op jit(solution)/shard_map/ppermute | solution.py:335
  9.9 4.2 %pack.6 = (f32[8,128,128]{2,1,0:T(8,128)}, f32[8,128,128]{2,1,0:T(8,128)}, f32[8,128,128]{2,1,0:T(8,128)}, f32[8,128,128]{2,1,0:T(8,128)}) custom-call(f32[4,2048,256]{2,1,0:T(8,128)} %bitcast.12, f32[4,2048,256]{2,1,0:T(8,128)} %bitcast.13), custom_call_target="tpu_custom_call" | custom-call | flops 1048576 | bytes 4194304 | tf_op jit(solution)/shard_map/pack/pallas_call | solution.py:52
  16.2 4.2 %pack.5 = (f32[8,128,128]{2,1,0:T(8,128)}, f32[8,128,128]{2,1,0:T(8,128)}, f32[8,128,128]{2,1,0:T(8,128)}, f32[8,128,128]{2,1,0:T(8,128)}) custom-call(f32[4,2048,256]{2,1,0:T(8,128)} %bitcast.14, f32[4,2048,256]{2,1,0:T(8,128)} %bitcast.15), custom_call_target="tpu_custom_call" | custom-call | flops 1048576 | bytes 4194304 | tf_op jit(solution)/shard_map/pack/pallas_call | solution.py:52
  22.6 4.2 %pack.4 = (f32[6,128,128]{2,1,0:T(8,128)}, f32[6,128,128]{2,1,0:T(8,128)}, f32[6,128,128]{2,1,0:T(8,128)}, f32[6,128,128]{2,1,0:T(8,128)}, f32[2,128,128]{2,1,0:...) custom-call(f32[4,2048,256]{2,1,0:T(8,128)} %bitcast.16, f32[4,2048,256]{2,1,0:T(8,128)} %bitcast.17), custom_call_target="tpu_custom_call" | custom-call | flops 1048576 | bytes 4194304 | tf_op jit(solution)/shard_map/pack/pallas_call | solution.py:52
  26.9 5.4 %collective-permute-done.14.refs_3_ = f32[8,128,128]{2,1,0:T(8,128)} collective-permute-done((f32[8,128,128]{2,1,0:T(8,128)}, f32[8,128,128]{2,1,0:T(8,128)}, u32[]{:S(2)}, u32[]{:S(2)}) %collective-permute-start.14) | collective-permute-done | bytes 524320 | tf_op jit(solution)/shard_map/ppermute | solution.py:335
  33.3 8.7 %collective-permute-done.10.refs_2_ = f32[8,128,128]{2,1,0:T(8,128)S(1)} collective-permute-done((f32[8,128,128]{2,1,0:T(8,128)}, f32[8,128,128]{2,1,0:T(8,128)S(1)}, u32[]{:S(2)}, u32[]{:S(2)}) %collective-permute-start.10) | collective-permute-done | bytes 524320 | tf_op jit(solution)/shard_map/ppermute | solution.py:335
  42.1 2.4 %collective-permute-start.8 = (f32[8,128,128]{2,1,0:T(8,128)}, f32[8,128,128]{2,1,0:T(8,128)S(1)}, u32[]{:S(2)}, u32[]{:S(2)}) collective-permute-start(f32[8,128,128]{2,1,0:T(8,128)} %get-tuple-element.44), channel_id=1, source_target_pairs={{0,2},{1,3},{2,0},{3,1},{4,6},{5,7},{6,4},{7,5},{8,10},{9,11},{10,... | collective-permute-start | bytes 1572872 | tf_op jit(solution)/shard_map/ppermute | solution.py:335
  45.6 6.1 %gram.5 = (f32[1280,128]{1,0:T(8,128)S(1)}, f32[4,1024,64]{2,1,0:T(8,128)}) custom-call(f32[8,128,128]{2,1,0:T(8,128)S(1)} %copy-done.4, f32[8,128,128]{2,1,0:T(8,128)S(1)} %collective-permute-done.12.refs_1_, f32[8,128,128]{2,1,0:T(8,128)S(1)} %copy-done.6, f32[8,128,128]{2,1,0:T(8,128)} %collective-permute-done.14.refs_3_, f32[64,512]{1,0:T(8,128)S(1)} %bitcast.5), custom_call_target="tpu_custom_call" | custom-call | flops 3221225472 | bytes 4194304 | tf_op jit(solution)/shard_map/gram/pallas_call | solution.py:171
  51.7 3.5 %collective-permute-start.3 = (f32[6,128,128]{2,1,0:T(8,128)S(1)}, f32[6,128,128]{2,1,0:T(8,128)S(1)}, u32[]{:S(2)}, u32[]{:S(2)}) collective-permute-start(f32[6,128,128]{2,1,0:T(8,128)S(1)} %copy-done.12), channel_id=1, source_target_pairs={{0,1},{1,2},{2,3},{3,0},{4,5},{5,6},{6,7},{7,4},{8,9},{9,10},{10,1... | collective-permute-start | bytes 1179656 | tf_op jit(solution)/shard_map/ppermute | solution.py:335
  55.8 12.0 %collective-permute-done.6.refs_1_ = f32[8,128,128]{2,1,0:T(8,128)S(1)} collective-permute-done((f32[8,128,128]{2,1,0:T(8,128)}, f32[8,128,128]{2,1,0:T(8,128)S(1)}, u32[]{:S(2)}, u32[]{:S(2)}) %collective-permute-start.6) | collective-permute-done | bytes 524320 | tf_op jit(solution)/shard_map/ppermute | solution.py:335
  68.5 5.1 %gram.6 = (f32[1280,128]{1,0:T(8,128)S(1)}, f32[4,1024,64]{2,1,0:T(8,128)}) custom-call(f32[8,128,128]{2,1,0:T(8,128)S(1)} %copy-done.3, f32[8,128,128]{2,1,0:T(8,128)S(1)} %collective-permute-done.9.refs_1_, f32[8,128,128]{2,1,0:T(8,128)S(1)} %collective-permute-done.10.refs_2_, ...), custom_call_target="tpu_custom_call", output_to_operand_aliasing={{0}: (5, {}), {1}: (6, {})} | custom-call | flops 3221225472 | bytes 4194304 | tf_op jit(solution)/shard_map/gram/pallas_call | solution.py:171
  73.6 3.6 %collective-permute-done.8.refs_3_ = f32[8,128,128]{2,1,0:T(8,128)S(1)} collective-permute-done((f32[8,128,128]{2,1,0:T(8,128)}, f32[8,128,128]{2,1,0:T(8,128)S(1)}, u32[]{:S(2)}, u32[]{:S(2)}) %collective-permute-start.8) | collective-permute-done | bytes 524320 | tf_op jit(solution)/shard_map/ppermute | solution.py:335
  78.3 5.0 %gram.7 = (f32[1280,128]{1,0:T(8,128)S(1)}, f32[4,1024,64]{2,1,0:T(8,128)}) custom-call(f32[8,128,128]{2,1,0:T(8,128)S(1)} %copy-done.2, f32[8,128,128]{2,1,0:T(8,128)S(1)} %collective-permute-done.6.refs_1_, f32[8,128,128]{2,1,0:T(8,128)S(1)} %collective-permute-done.7.refs_2_, ...), custom_call_target="tpu_custom_call", output_to_operand_aliasing={{0}: (5, {}), {1}: (6, {})} | custom-call | flops 3221225472 | bytes 4194304 | tf_op jit(solution)/shard_map/gram/pallas_call | solution.py:171
  83.3 4.0 %collective-permute-done.3.refs_1_ = f32[6,128,128]{2,1,0:T(8,128)S(1)} collective-permute-done((f32[6,128,128]{2,1,0:T(8,128)S(1)}, f32[6,128,128]{2,1,0:T(8,128)S(1)}, u32[]{:S(2)}, u32[]{:S(2)}) %collective-permute-start.3) | collective-permute-done | bytes 393248 | tf_op jit(solution)/shard_map/ppermute | solution.py:335
  87.9 6.1 %collective-permute-done.5.refs_3_ = f32[6,128,128]{2,1,0:T(8,128)S(1)} collective-permute-done((f32[6,128,128]{2,1,0:T(8,128)S(1)}, f32[6,128,128]{2,1,0:T(8,128)S(1)}, u32[]{:S(2)}, u32[]{:S(2)}) %collective-permute-start.5) | collective-permute-done | bytes 393248 | tf_op jit(solution)/shard_map/ppermute | solution.py:335
  94.0 4.8 %gram.8 = (f32[1280,128]{1,0:T(8,128)S(1)}, f32[4,1024,64]{2,1,0:T(8,128)}) custom-call(f32[6,128,128]{2,1,0:T(8,128)S(1)} %copy-done.7, f32[6,128,128]{2,1,0:T(8,128)S(1)} %collective-permute-done.3.refs_1_, f32[6,128,128]{2,1,0:T(8,128)S(1)} %collective-permute-done.4.refs_2_, ...), custom_call_target="tpu_custom_call", output_to_operand_aliasing={{0}: (5, {}), {1}: (6, {})} | custom-call | flops 2415919104 | bytes 3145728 | tf_op jit(solution)/shard_map/gram/pallas_call | solution.py:171
  99.5 3.1 %gram.9 = (f32[640,128]{1,0:T(8,128)S(1)}, f32[640,128]{1,0:T(8,128)S(1)}, f32[4,1024,64]{2,1,0:T(8,128)}) custom-call(f32[2,128,128]{2,1,0:T(8,128)S(1)} %copy-done.1, f32[2,128,128]{2,1,0:T(8,128)S(1)} %collective-permute-done.refs_1_, f32[2,128,128]{2,1,0:T(8,128)S(1)} %collective-permute-done.1.refs_2_, ...), custom_call_target="tpu_custom_call", output_to_operand_aliasing={{2}: (6, {})} | custom-call | flops 805306368 | bytes 1048576 | tf_op jit(solution)/shard_map/gram/pallas_call | solution.py:171
  102.5 2.0 %collective-permute-start.15 = (f32[640,128]{1,0:T(8,128)S(1)}, f32[640,128]{1,0:T(8,128)S(1)}, u32[]{:S(2)}, u32[]{:S(2)}) collective-permute-start(f32[640,128]{1,0:T(8,128)S(1)} %get-tuple-element.62), channel_id=1, source_target_pairs={{0,4},{4,0},{1,5},{5,1},{2,6},{6,2},{3,7},{7,3},{8,12},{12,8},{9,1... | collective-permute-start | bytes 983048 | tf_op jit(solution)/shard_map/ppermute | solution.py:191
  105.9 16.4 %all_to_all.10 = f32[16,40,128]{2,1,0:T(8,128)S(1)} all-to-all(f32[16,40,128]{2,1,0:T(8,128)S(1)} %bitcast.21), channel_id=1, replica_groups=mesh['z'=4,'y'=4,'core'=2,'narrow'=4] {'z','y'}, dimensions={0} | all-to-all | bytes 655360 | tf_op jit(solution)/shard_map/all_to_all | solution.py:193
  125.0 2.0 %collective-permute-start.17 = (f32[40,128]{1,0:T(8,128)S(1)}, f32[40,128]{1,0:T(8,128)S(1)}, u32[]{:S(2)}, u32[]{:S(2)}) collective-permute-start(f32[40,128]{1,0:T(8,128)S(1)} %add.10), channel_id=1, source_target_pairs={{0,3},{1,2},{2,1},{3,0},{4,7},{5,6},{6,5},{7,4},{8,11},{9,10},{10,... | collective-permute-start | bytes 61448 | tf_op jit(solution)/shard_map/ppermute | solution.py:197
  128.9 10.7 %all_to_all.11 = f32[16,40,128]{2,1,0:T(8,128)S(1)} all-to-all(f32[16,40,128]{2,1,0:T(8,128)S(1)} %broadcast_in_dim.2), channel_id=1, replica_groups=mesh['z'=4,'y'=4,'core'=2,'narrow'=4] {'z','y'}, dimensions={0} | all-to-all | bytes 655360 | tf_op jit(solution)/shard_map/all_to_all | solution.py:193
  139.6 5.0 %collective-permute-start.18 = (f32[640,128]{1,0:T(8,128)S(1)}, f32[640,128]{1,0:T(8,128)S(1)}, u32[]{:S(2)}, u32[]{:S(2)}) collective-permute-start(f32[640,128]{1,0:T(8,128)S(1)} %bitcast.19), channel_id=1, source_target_pairs={{0,4},{4,0},{1,5},{5,1},{2,6},{6,2},{3,7},{7,3},{8,12},{12,8},{9,1... | collective-permute-start | bytes 983048 | tf_op jit(solution)/shard_map/ppermute | solution.py:199
  146.6 14.2 %upper_factor.1 = f32[512,512]{1,0:T(8,128)} custom-call(f32[640,128]{1,0:T(8,128)} %bitcast.20, f32[640,128]{1,0:T(8,128)} %copy-done.9), custom_call_target="tpu_custom_call" | custom-call | tf_op jit(solution)/shard_map/upper_factor/pallas_call | solution.py:309
  (63 shorter events, 21.1 us)
Async XLA Ops:
  4.8 15.6 %collective-permute-start.12 = (f32[8,128,128]{2,1,0:T(8,128)}, f32[8,128,128]{2,1,0:T(8,128)S(1)}, u32[]{:S(2)}, u32[]{:S(2)}) collective-permute-start(f32[8,128,128]{2,1,0:T(8,128)} %get-tuple-element.50), channel_id=1, source_target_pairs={{0,1},{1,2},{2,3},{3,0},{4,5},{5,6},{6,7},{7,4},{8,9},{9,10},{10,1... | collective-permute-start | bytes 1572872 | tf_op jit(solution)/shard_map/ppermute | solution.py:335
  6.9 13.5 %collective-permute-start.13 = (f32[8,128,128]{2,1,0:T(8,128)}, f32[8,128,128]{2,1,0:T(8,128)S(1)}, u32[]{:S(2)}, u32[]{:S(2)}) collective-permute-start(f32[8,128,128]{2,1,0:T(8,128)} %get-tuple-element.51), channel_id=1, source_target_pairs={{0,3},{1,0},{2,1},{3,2},{4,7},{5,4},{6,5},{7,6},{8,11},{9,8},{10,9... | collective-permute-start | bytes 1572872 | tf_op jit(solution)/shard_map/ppermute | solution.py:335
  8.1 24.1 %collective-permute-start.14 = (f32[8,128,128]{2,1,0:T(8,128)}, f32[8,128,128]{2,1,0:T(8,128)}, u32[]{:S(2)}, u32[]{:S(2)}) collective-permute-start(f32[8,128,128]{2,1,0:T(8,128)} %get-tuple-element.52), channel_id=1, source_target_pairs={{0,2},{1,3},{2,0},{3,1},{4,6},{5,7},{6,4},{7,5},{8,10},{9,11},{10,... | collective-permute-start | bytes 1572872 | tf_op jit(solution)/shard_map/ppermute | solution.py:335
  14.1 28.0 %collective-permute-start.10 = (f32[8,128,128]{2,1,0:T(8,128)}, f32[8,128,128]{2,1,0:T(8,128)S(1)}, u32[]{:S(2)}, u32[]{:S(2)}) collective-permute-start(f32[8,128,128]{2,1,0:T(8,128)} %get-tuple-element.47), channel_id=1, source_target_pairs={{0,3},{1,0},{2,1},{3,2},{4,7},{5,4},{6,5},{7,6},{8,11},{9,8},{10,9... | collective-permute-start | bytes 1572872 | tf_op jit(solution)/shard_map/ppermute | solution.py:335
  15.0 36.7 %collective-permute-start.11 = (f32[8,128,128]{2,1,0:T(8,128)}, f32[8,128,128]{2,1,0:T(8,128)S(1)}, u32[]{:S(2)}, u32[]{:S(2)}) collective-permute-start(f32[8,128,128]{2,1,0:T(8,128)} %get-tuple-element.48), channel_id=1, source_target_pairs={{0,2},{1,3},{2,0},{3,1},{4,6},{5,7},{6,4},{7,5},{8,10},{9,11},{10,... | collective-permute-start | bytes 1572872 | tf_op jit(solution)/shard_map/ppermute | solution.py:335
  20.4 35.2 %collective-permute-start.9 = (f32[8,128,128]{2,1,0:T(8,128)}, f32[8,128,128]{2,1,0:T(8,128)S(1)}, u32[]{:S(2)}, u32[]{:S(2)}) collective-permute-start(f32[8,128,128]{2,1,0:T(8,128)} %get-tuple-element.46), channel_id=1, source_target_pairs={{0,1},{1,2},{2,3},{3,0},{4,5},{5,6},{6,7},{7,4},{8,9},{9,10},{10,1... | collective-permute-start | bytes 1572872 | tf_op jit(solution)/shard_map/ppermute | solution.py:335
  21.3 23.3 %copy-start = (f32[512,64]{0,1:T(8,128)S(1)}, f32[512,64]{0,1:T(8,128)}, u32[]{:S(2)}) copy-start(f32[512,64]{0,1:T(8,128)} %param.3) | copy-start | bytes 393220
  21.3 23.3 %copy-start.4 = (f32[8,128,128]{2,1,0:T(8,128)S(1)}, f32[8,128,128]{2,1,0:T(8,128)}, u32[]{:S(2)}) copy-start(f32[8,128,128]{2,1,0:T(8,128)} %get-tuple-element.49.refs_0_) | copy-start | bytes 1572868
  21.3 46.6 %collective-permute-start.6 = (f32[8,128,128]{2,1,0:T(8,128)}, f32[8,128,128]{2,1,0:T(8,128)S(1)}, u32[]{:S(2)}, u32[]{:S(2)}) collective-permute-start(f32[8,128,128]{2,1,0:T(8,128)} %get-tuple-element.42), channel_id=1, source_target_pairs={{0,1},{1,2},{2,3},{3,0},{4,5},{5,6},{6,7},{7,4},{8,9},{9,10},{10,1... | collective-permute-start | bytes 1572872 | tf_op jit(solution)/shard_map/ppermute | solution.py:335
  32.2 41.3 %collective-permute-start.7 = (f32[8,128,128]{2,1,0:T(8,128)}, f32[8,128,128]{2,1,0:T(8,128)S(1)}, u32[]{:S(2)}, u32[]{:S(2)}) collective-permute-start(f32[8,128,128]{2,1,0:T(8,128)} %get-tuple-element.43), channel_id=1, source_target_pairs={{0,3},{1,0},{2,1},{3,2},{4,7},{5,4},{6,5},{7,6},{8,11},{9,8},{10,9... | collective-permute-start | bytes 1572872 | tf_op jit(solution)/shard_map/ppermute | solution.py:335
  42.1 35.0 %collective-permute-start.8 = (f32[8,128,128]{2,1,0:T(8,128)}, f32[8,128,128]{2,1,0:T(8,128)S(1)}, u32[]{:S(2)}, u32[]{:S(2)}) collective-permute-start(f32[8,128,128]{2,1,0:T(8,128)} %get-tuple-element.44), channel_id=1, source_target_pairs={{0,2},{1,3},{2,0},{3,1},{4,6},{5,7},{6,4},{7,5},{8,10},{9,11},{10,... | collective-permute-start | bytes 1572872 | tf_op jit(solution)/shard_map/ppermute | solution.py:335
  45.6 22.3 %copy-start.10 = (f32[6,128,128]{2,1,0:T(8,128)S(1)}, f32[6,128,128]{2,1,0:T(8,128)}, u32[]{:S(2)}) copy-start(f32[6,128,128]{2,1,0:T(8,128)} %get-tuple-element.40) | copy-start | bytes 1179652
  45.6 22.9 %copy-start.3 = (f32[8,128,128]{2,1,0:T(8,128)S(1)}, f32[8,128,128]{2,1,0:T(8,128)}, u32[]{:S(2)}) copy-start(f32[8,128,128]{2,1,0:T(8,128)} %get-tuple-element.45.refs_0_) | copy-start | bytes 1572868
  51.7 35.6 %collective-permute-start.3 = (f32[6,128,128]{2,1,0:T(8,128)S(1)}, f32[6,128,128]{2,1,0:T(8,128)S(1)}, u32[]{:S(2)}, u32[]{:S(2)}) collective-permute-start(f32[6,128,128]{2,1,0:T(8,128)S(1)} %copy-done.12), channel_id=1, source_target_pairs={{0,1},{1,2},{2,3},{3,0},{4,5},{5,6},{6,7},{7,4},{8,9},{9,10},{10,1... | collective-permute-start | bytes 1179656 | tf_op jit(solution)/shard_map/ppermute | solution.py:335
  55.6 32.3 %collective-permute-start.4 = (f32[6,128,128]{2,1,0:T(8,128)S(1)}, f32[6,128,128]{2,1,0:T(8,128)S(1)}, u32[]{:S(2)}, u32[]{:S(2)}) collective-permute-start(f32[6,128,128]{2,1,0:T(8,128)S(1)} %copy-done.11), channel_id=1, source_target_pairs={{0,3},{1,0},{2,1},{3,2},{4,7},{5,4},{6,5},{7,6},{8,11},{9,8},{10,9... | collective-permute-start | bytes 1179656 | tf_op jit(solution)/shard_map/ppermute | solution.py:335
  67.9 26.2 %collective-permute-start.5 = (f32[6,128,128]{2,1,0:T(8,128)S(1)}, f32[6,128,128]{2,1,0:T(8,128)S(1)}, u32[]{:S(2)}, u32[]{:S(2)}) collective-permute-start(f32[6,128,128]{2,1,0:T(8,128)S(1)} %copy-done.10), channel_id=1, source_target_pairs={{0,2},{1,3},{2,0},{3,1},{4,6},{5,7},{6,4},{7,5},{8,10},{9,11},{10,... | collective-permute-start | bytes 1179656 | tf_op jit(solution)/shard_map/ppermute | solution.py:335
  73.6 25.2 %collective-permute-start = (f32[2,128,128]{2,1,0:T(8,128)S(1)}, f32[2,128,128]{2,1,0:T(8,128)S(1)}, u32[]{:S(2)}, u32[]{:S(2)}) collective-permute-start(f32[2,128,128]{2,1,0:T(8,128)S(1)} %copy-done.15), channel_id=1, source_target_pairs={{0,1},{1,2},{2,3},{3,0},{4,5},{5,6},{6,7},{7,4},{8,9},{9,10},{10,1... | collective-permute-start | bytes 393224 | tf_op jit(solution)/shard_map/ppermute | solution.py:335
  77.1 21.7 %collective-permute-start.1 = (f32[2,128,128]{2,1,0:T(8,128)S(1)}, f32[2,128,128]{2,1,0:T(8,128)S(1)}, u32[]{:S(2)}, u32[]{:S(2)}) collective-permute-start(f32[2,128,128]{2,1,0:T(8,128)S(1)} %copy-done.14), channel_id=1, source_target_pairs={{0,3},{1,0},{2,1},{3,2},{4,7},{5,4},{6,5},{7,6},{8,11},{9,8},{10,9... | collective-permute-start | bytes 393224 | tf_op jit(solution)/shard_map/ppermute | solution.py:335
  78.3 15.7 %copy-start.7 = (f32[6,128,128]{2,1,0:T(8,128)S(1)}, f32[6,128,128]{2,1,0:T(8,128)}, u32[]{:S(2)}) copy-start(f32[6,128,128]{2,1,0:T(8,128)} %get-tuple-element.37.refs_0_) | copy-start | bytes 1179652
  87.3 12.2 %collective-permute-start.2 = (f32[2,128,128]{2,1,0:T(8,128)S(1)}, f32[2,128,128]{2,1,0:T(8,128)S(1)}, u32[]{:S(2)}, u32[]{:S(2)}) collective-permute-start(f32[2,128,128]{2,1,0:T(8,128)S(1)} %copy-done.13), channel_id=1, source_target_pairs={{0,2},{1,3},{2,0},{3,1},{4,6},{5,7},{6,4},{7,5},{8,10},{9,11},{10,... | collective-permute-start | bytes 393224 | tf_op jit(solution)/shard_map/ppermute | solution.py:335
  102.5 3.3 %collective-permute-start.15 = (f32[640,128]{1,0:T(8,128)S(1)}, f32[640,128]{1,0:T(8,128)S(1)}, u32[]{:S(2)}, u32[]{:S(2)}) collective-permute-start(f32[640,128]{1,0:T(8,128)S(1)} %get-tuple-element.62), channel_id=1, source_target_pairs={{0,4},{4,0},{1,5},{5,1},{2,6},{6,2},{3,7},{7,3},{8,12},{12,8},{9,1... | collective-permute-start | bytes 983048 | tf_op jit(solution)/shard_map/ppermute | solution.py:191
  122.3 2.7 %collective-permute-start.16 = (f32[40,128]{1,0:T(8,128)S(1)}, f32[40,128]{1,0:T(8,128)S(1)}, u32[]{:S(2)}, u32[]{:S(2)}) collective-permute-start(f32[40,128]{1,0:T(8,128)S(1)} %reduce_sum.9), channel_id=1, source_target_pairs={{0,1},{1,0},{2,3},{3,2},{4,5},{5,4},{6,7},{7,6},{8,9},{9,8},{10,11... | collective-permute-start | bytes 61448 | tf_op jit(solution)/shard_map/ppermute | solution.py:197
  125.0 3.8 %collective-permute-start.17 = (f32[40,128]{1,0:T(8,128)S(1)}, f32[40,128]{1,0:T(8,128)S(1)}, u32[]{:S(2)}, u32[]{:S(2)}) collective-permute-start(f32[40,128]{1,0:T(8,128)S(1)} %add.10), channel_id=1, source_target_pairs={{0,3},{1,2},{2,1},{3,0},{4,7},{5,6},{6,5},{7,4},{8,11},{9,10},{10,... | collective-permute-start | bytes 61448 | tf_op jit(solution)/shard_map/ppermute | solution.py:197
  139.6 6.3 %collective-permute-start.18 = (f32[640,128]{1,0:T(8,128)S(1)}, f32[640,128]{1,0:T(8,128)S(1)}, u32[]{:S(2)}, u32[]{:S(2)}) collective-permute-start(f32[640,128]{1,0:T(8,128)S(1)} %bitcast.19), channel_id=1, source_target_pairs={{0,4},{4,0},{1,5},{5,1},{2,6},{6,2},{3,7},{7,3},{8,12},{12,8},{9,1... | collective-permute-start | bytes 983048 | tf_op jit(solution)/shard_map/ppermute | solution.py:199
  (11 other events, 63.0 us)
